TPU v7x, 32 devices: a whole 2x2x4 slice. The times are simulated.
32 devices in a mesh: dp: 4 (over x, core), expert: 8 (over z, y).
Axes of the slice: x: 2, y: 2, z: 4, core: 2. Of those that a mesh axis runs over, the one named last changes fastest.
Arguments:
- dense_weights: bfloat16 [3, 5632, 2048], P(None, 'dp', 'expert'), may hold values from -0.125 to 0.125
- tokens: bfloat16 [1024, 2048], P('expert'), may hold values from -6 to 6
- cotangent: bfloat16 [1024, 2048], P('expert'), may hold values from -6 to 6
- routes: int32 [1024, 4], P('expert'), may hold values from 0 to 7, all different within a row; in each aligned block of 128 rows (0 to 127, 128 to 255, ...) at most 80 rows name the same one
- route_gates: float32 [1024, 4], P('expert'), may hold values from 0.2 to 1
- unit_perm: int32 [2, 5632], replicated, may hold values from 0 to 5631, as said below
- slab_owner: int32 [8], replicated, may hold values from 0 to 7, each once
Outputs:
- mixed: bfloat16 [1024, 2048], P('expert', 'dp')
- token_grad: bfloat16 [1024, 2048], P('expert', 'dp')
- expert_grad: bfloat16 [8, 3, 1408, 2048], P('expert', None, 'dp')
Inputs may be any that keep to these rules, and one draw needn't show every extreme that they name: `unit_perm`: each row is a permutation of the 5632 units. In every row, for every slab s and share g, the 352 positions s * 1408 + g * 352 up to s * 1408 + (g + 1) * 352 - 1 hold exactly 88 units of each block of 1408 consecutive units. `slab_owner`: each slab number c * 4 + s is owned by exactly one expert. `routes`: each row names 4 different experts. In each aligned block of 128 rows no expert is named more than 80 times, a bound that some block reaches.
All inputs are finite; a program needn't handle non-finite values.
Results may differ from a plain program's by a relative error of at most 0.013.
Values may be sent and summed in bfloat16 or wider, within the bound.
A program may use at most 128 MiB of HBM per device.

v0:
```python
import functools

import jax
import jax.numpy as jnp
from jax import lax
from jax.experimental import pallas as pl
from jax.experimental.pallas import tpu as pltpu
from jax.sharding import PartitionSpec as P

F32 = jnp.float32
BF16 = jnp.bfloat16


def silu_parts(preact):
    sigmoid_value = jax.nn.sigmoid(preact)
    return (preact * sigmoid_value, sigmoid_value * (1.0 + preact * (1.0 - sigmoid_value)))


def dot(left, right, left_dim, right_dim):
    return lax.dot_general(
        left, right, (((left_dim,), (right_dim,)), ((), ())), preferred_element_type=F32
    )


def block_ranks(blocks, block):
    width = blocks.shape[-1]
    mask = blocks == block
    upper = lax.broadcasted_iota(jnp.int32, (width, width), 0) < lax.broadcasted_iota(
        jnp.int32, (width, width), 1
    )
    rank = jnp.dot(mask.astype(BF16), upper.astype(BF16), preferred_element_type=F32)
    return mask, rank.astype(jnp.int32)


def log2(count):
    return count.bit_length() - 1


def flip(index, place):
    return index + (1 - 2 * (index // (1 << place) % 2)) * (1 << place)


def peer(device, n_ex):
    return {"dp": device // n_ex, "expert": device % n_ex}


STREAMS = 4


def halving_orders(dp_bits, ex_bits):
    rest = [ex_bits + bit for bit in range(1, dp_bits)] + list(range(ex_bits))
    turns = [[0, 1, 2], [1, 2, 0], [2, 0, 1], [1, 0, 2]]
    orders = []
    for turn in turns:
        head = [rest[at] for at in turn if at < len(rest)]
        orders.append([ex_bits] + head + rest[len(head) :])
    return orders


def halving_kernel(n_dp, n_ex, n_arrays, with_grads, *refs):
    ins, refs = refs[:n_arrays], refs[n_arrays:]
    acts, order_ref, fulls, refs = (
        (refs[:3], refs[3], refs[4:6], refs[6:]) if with_grads else ((), None, (), refs)
    )
    outs, refs = refs[:n_arrays], refs[n_arrays:]
    if with_grads:
        grads, full_rows, grad_rows, act_rows, full_sem, grad_sem = refs[0], *refs[-5:]
        refs = refs[1:-5]
    data, recv, load_sem, send_sem, recv_sem = refs
    me = lax.axis_index("dp") * n_ex + lax.axis_index("expert")
    bits = log2(n_dp) + log2(n_ex)
    orders = halving_orders(log2(n_dp), log2(n_ex))
    rows, part = data.shape[2:]
    splits = STREAMS // n_arrays

    for stream in range(STREAMS):
        source, at = ins[stream // splits], stream % splits
        for g in range(n_dp):

            def load(e, carry, source=source, at=at, g=g, stream=stream):
                start = pl.multiple_of(e * (rows * splits) + at * rows, rows)
                pltpu.make_async_copy(
                    source.at[pl.ds(start, rows), pl.ds(g * part, part)],
                    data.at[stream, g * n_ex + e],
                    load_sem.at[stream],
                ).start()
                return carry

            lax.fori_loop(0, n_ex, load, 0)

    for at, full in enumerate(fulls):
        pltpu.make_async_copy(full, full_rows.at[at], full_sem.at[at]).start()

    def weight_grad(k):
        if k != 1:
            at = k // 2
            pltpu.make_async_copy(fulls[at], full_rows.at[at], full_sem.at[at]).wait()
        width = full_rows.shape[-1]
        piece = min(512, width)
        act_rows[...] = dot(order_ref[...], acts[k][...], 1, 1).astype(BF16)

        def product(step, carry):
            lanes = pl.ds(pl.multiple_of(step * piece, piece), piece)
            grad_rows[k, :, lanes] = jnp.dot(
                act_rows[...], full_rows[k // 2, :, lanes], preferred_element_type=F32
            ).astype(BF16)
            return carry

        lax.fori_loop(0, width // piece, product, 0)
        pltpu.make_async_copy(grad_rows.at[k], grads.at[0, k], grad_sem.at[k]).start()

    barrier = pltpu.get_barrier_semaphore()
    for place in range(bits):
        pl.semaphore_signal(
            barrier,
            inc=1,
            device_id=peer(flip(me, place), n_ex),
            device_id_type=pl.DeviceIdType.MESH,
        )
    pl.semaphore_wait(barrier, bits)

    def block_of(stream, step, choice, sent):
        order = orders[stream]
        index = 0
        for place in order[: step + 1]:
            index = index + me // (1 << place) % 2 * (1 << place)
        if sent:
            index = flip(index, order[step])
        for bit, place in enumerate(sorted(order[step + 1 :])):
            index = index + choice // (1 << bit) % 2 * (1 << place)
        return index

    def count(step):
        return 1 << (bits - 1 - step)

    def offset(step):
        return (1 << bits) - (1 << (bits - step))

    def send(stream, step, choice):
        pltpu.make_async_remote_copy(
            src_ref=data.at[stream, block_of(stream, step, choice, True)],
            dst_ref=recv.at[stream, offset(step) + choice],
            send_sem=send_sem.at[stream, step],
            recv_sem=recv_sem.at[stream, step],
            device_id=peer(flip(me, orders[stream][step]), n_ex),
            device_id_type=pl.DeviceIdType.MESH,
        ).start()

    def region(stream, step):
        view = recv.at[stream, pl.ds(offset(step), count(step))]
        return pltpu.make_async_remote_copy(
            src_ref=view,
            dst_ref=view,
            send_sem=send_sem.at[stream, step],
            recv_sem=recv_sem.at[stream, step],
            device_id=peer(flip(me, orders[stream][step]), n_ex),
            device_id_type=pl.DeviceIdType.MESH,
        )

    def number(stream, step, choice, sent):
        order = orders[stream]
        later = sorted(order[step + 1 :])
        place = order[step + 1]
        mine = me // (1 << place) % 2
        value = (1 - mine if sent else mine) * (1 << later.index(place))
        for bit, other in enumerate(sorted(order[step + 2 :])):
            value = value + choice // (1 << bit) % 2 * (1 << later.index(other))
        return value

    for stream in range(STREAMS):
        pltpu.make_async_copy(data.at[stream], data.at[stream], load_sem.at[stream]).wait()

        def first(choice, carry, stream=stream):
            send(stream, 0, choice)
            return carry

        lax.fori_loop(0, count(0), first, 0)

    if with_grads:
        weight_grad(0)
    for step in range(bits):
        for stream in range(STREAMS):
            region(stream, step).wait_recv()
            if step == bits - 1:
                total = data[stream, me].astype(F32) + recv[stream, offset(step)].astype(F32)
                outs[stream // splits][pl.ds(stream % splits * rows, rows), :] = total.astype(BF16)
                continue
            for sent in (True, False):

                def add(choice, carry, stream=stream, step=step, sent=sent):
                    block = block_of(stream, step + 1, choice, sent)
                    slot = offset(step) + number(stream, step, choice, sent)
                    total = data[stream, block].astype(F32) + recv[stream, slot].astype(F32)
                    data[stream, block] = total.astype(BF16)
                    if sent:
                        send(stream, step + 1, choice)
                    return carry

                lax.fori_loop(0, count(step + 1), add, 0)
        if step < 2 and with_grads:
            weight_grad(step + 1)

    if with_grads:
        for k in range(3):
            pltpu.make_async_copy(grad_rows.at[k], grads.at[0, k], grad_sem.at[k]).wait()
    for step in range(bits):
        for stream in range(STREAMS):
            region(stream, step).wait_send()


def halving_sum(n_dp, n_ex, arrays, acts=(), fulls=()):
    total, width = arrays[0].shape
    tok, part, n_arrays = total // n_ex, width // n_dp, len(arrays)
    rows = tok * n_arrays // STREAMS
    blocks = n_dp * n_ex
    steps = log2(blocks)
    any_spec, vmem_spec = pl.BlockSpec(memory_space=pl.ANY), pl.BlockSpec(memory_space=pltpu.VMEM)
    out_shape = [jax.ShapeDtypeStruct((tok, part), BF16)] * n_arrays
    out_specs = [vmem_spec] * n_arrays
    scratch = [
        pltpu.VMEM((STREAMS, blocks, rows, part), BF16),
        pltpu.VMEM((STREAMS, blocks - 1, rows, part), BF16),
        pltpu.SemaphoreType.DMA((STREAMS,)),
        pltpu.SemaphoreType.DMA((STREAMS, steps)),
        pltpu.SemaphoreType.DMA((STREAMS, steps)),
    ]
    if acts:
        share = acts[0].shape[1]
        out_shape = out_shape + [jax.ShapeDtypeStruct((1, 3, share, width), BF16)]
        out_specs = out_specs + [any_spec]
        scratch = scratch + [
            pltpu.VMEM((2, total, width), BF16),
            pltpu.VMEM((3, share, width), BF16),
            pltpu.VMEM((share, total), BF16),
            pltpu.SemaphoreType.DMA((2,)),
            pltpu.SemaphoreType.DMA((3,)),
        ]
    return pl.pallas_call(
        functools.partial(halving_kernel, n_dp, n_ex, n_arrays, bool(acts)),
        out_shape=out_shape,
        in_specs=[any_spec] * n_arrays + [vmem_spec] * len(acts) + [any_spec] * len(fulls),
        out_specs=out_specs,
        scratch_shapes=scratch,
        compiler_params=pltpu.CompilerParams(
            collective_id=1, has_side_effects=True, vmem_limit_bytes=60 << 20
        ),
        name="halving_sum",
    )(*arrays, *acts, *fulls)


def flip_mask(index, mask):
    place = 0
    while mask >> place:
        if mask >> place & 1:
            index = flip(index, place)
        place += 1
    return index


def gather_kernel(
    n_dp, n_ex, picked, tokens, cotangent, table, weights, all_x, all_c, gates, load_sem, row_sem, tok_send, tok_recv
):
    row, col = lax.axis_index("dp"), lax.axis_index("expert")
    me = row * n_ex + col
    blocks, pick, wide = picked.shape
    feat = wide // 3
    tok, width = tokens.shape
    part = width // n_dp
    dp_bits, ex_bits = log2(n_dp), log2(n_ex)
    ex_order = list(range(ex_bits - 1, -1, -1))
    dp_order = [ex_bits + bit for bit in range(dp_bits - 1, -1, -1)]
    orders = [ex_order + dp_order, ex_order + dp_order]
    if dp_bits > 1:
        orders[1] = ex_order[:-1] + [dp_order[0], ex_order[-1]] + dp_order[1:]
    fulls = (all_x, all_c)

    def place(full, device):
        return full.at[
            pl.ds(pl.multiple_of(device % n_ex * tok, tok), tok),
            pl.ds(pl.multiple_of(device // n_ex * part, part), part),
        ]

    for at, (source, full) in enumerate(((tokens, all_x), (cotangent, all_c))):
        pltpu.make_async_copy(
            source.at[:, pl.ds(pl.multiple_of(row * part, part), part)], place(full, me), load_sem.at[at]
        ).start()

    def spot(k):
        return weights.at[
            k,
            pl.ds(pl.multiple_of(row * pick, 8), pick),
            pl.ds(pl.multiple_of(col * feat, feat), feat),
        ]

    for k in range(3):
        pltpu.make_async_copy(
            picked.at[me, :, pl.ds(k * feat, feat)], spot(k), row_sem.at[1]
        ).start()
    pltpu.make_async_copy(table.at[col], gates.at[col], row_sem.at[3]).start()

    barrier = pltpu.get_barrier_semaphore()
    for mask in range(1, blocks):
        pl.semaphore_signal(
            barrier,
            inc=1,
            device_id=peer(flip_mask(me, mask), n_ex),
            device_id_type=pl.DeviceIdType.MESH,
        )
    pl.semaphore_wait(barrier, blocks - 1)
    for at, full in enumerate(fulls):
        pltpu.make_async_copy(place(full, me), place(full, me), load_sem.at[at]).wait()

    def send_tokens(at, step):
        full, order = fulls[at], orders[at]

        def one(choice, carry):
            device = me
            for bit, other in enumerate(order[:step]):
                mine = me // (1 << other) % 2
                device = device + (choice // (1 << bit) % 2 - mine) * (1 << other)
            pltpu.make_async_remote_copy(
                src_ref=place(full, device),
                dst_ref=place(full, device),
                send_sem=tok_send.at[at, step],
                recv_sem=tok_recv.at[at, step],
                device_id=peer(flip(me, order[step]), n_ex),
                device_id_type=pl.DeviceIdType.MESH,
            ).start()
            return carry

        lax.fori_loop(0, 1 << step, one, 0)

    def wait_tokens(at, step, sem):
        rows = min(1 << step, n_ex)
        view = fulls[at].at[pl.ds(0, rows * tok), pl.ds(0, (1 << step) // rows * part)]
        pltpu.make_async_copy(view, view, sem.at[at, step]).wait()

    def send_rows(mask):
        device = flip_mask(me, mask)
        for k in range(3):
            pltpu.make_async_remote_copy(
                src_ref=picked.at[device, :, pl.ds(k * feat, feat)],
                dst_ref=spot(k),
                send_sem=row_sem.at[0],
                recv_sem=row_sem.at[1],
                device_id=peer(device, n_ex),
                device_id_type=pl.DeviceIdType.MESH,
            ).start()

    steps = dp_bits + ex_bits
    masks = [at * 11 % blocks for at in range(1, blocks)]
    chunk = -(-len(masks) // steps)
    for mask in range(1, n_ex):
        device = flip_mask(me, mask)
        pltpu.make_async_remote_copy(
            src_ref=table.at[device % n_ex],
            dst_ref=gates.at[col],
            send_sem=row_sem.at[2],
            recv_sem=row_sem.at[3],
            device_id=peer(device, n_ex),
            device_id_type=pl.DeviceIdType.MESH,
        ).start()
    for step in range(steps):
        for at in range(2):
            if step:
                wait_tokens(at, step - 1, tok_recv)
            send_tokens(at, step)
        for mask in masks[step * chunk : (step + 1) * chunk]:
            send_rows(mask)

    for at in range(2):
        wait_tokens(at, steps - 1, tok_recv)
        for step in range(steps):
            wait_tokens(at, step, tok_send)
    sent = picked.at[pl.ds(0, blocks - 1)]
    pltpu.make_async_copy(sent, sent, row_sem.at[0]).wait()
    pltpu.make_async_copy(weights, weights, row_sem.at[1]).wait()
    sent = table.at[pl.ds(0, n_ex - 1)]
    pltpu.make_async_copy(sent, sent, row_sem.at[2]).wait()
    pltpu.make_async_copy(gates, gates, row_sem.at[3]).wait()


def gather_all(n_dp, n_ex, picked, tokens, cotangent, table):
    blocks, pick, wide = picked.shape
    tok, width = tokens.shape
    steps = log2(blocks)
    table = table.reshape(n_ex, 1, tok)
    return pl.pallas_call(
        functools.partial(gather_kernel, n_dp, n_ex),
        out_shape=[
            jax.ShapeDtypeStruct((3, n_dp * pick, width), BF16),
            jax.ShapeDtypeStruct((n_ex * tok, width), BF16),
            jax.ShapeDtypeStruct((n_ex * tok, width), BF16),
            jax.ShapeDtypeStruct((n_ex, 1, tok), F32),
        ],
        in_specs=[pl.BlockSpec(memory_space=pltpu.VMEM)] * 4,
        out_specs=[pl.BlockSpec(memory_space=pl.ANY)] * 3
        + [pl.BlockSpec(memory_space=pltpu.VMEM)],
        scratch_shapes=[
            pltpu.SemaphoreType.DMA((2,)),
            pltpu.SemaphoreType.DMA((4,)),
            pltpu.SemaphoreType.DMA((2, steps)),
            pltpu.SemaphoreType.DMA((2, steps)),
        ],
        compiler_params=pltpu.CompilerParams(
            collective_id=2, has_side_effects=True, vmem_limit_bytes=60 << 20
        ),
        name="gather_all",
    )(picked, tokens, cotangent, table)


def gather_plain(n_dp, n_ex, row, picked, tokens, cotangent, table):
    _, pick, wide = picked.shape
    tok, width = tokens.shape
    arrived = lax.all_to_all(picked, ("dp", "expert"), split_axis=0, concat_axis=0, tiled=True)
    arrived = arrived.reshape(n_dp, n_ex, pick, 3, wide // 3)
    weights = jnp.transpose(arrived, (3, 0, 2, 1, 4)).reshape(3, n_dp * pick, width)
    part = width // n_dp
    both = jnp.concatenate(
        [
            lax.dynamic_slice(tokens, (0, row * part), (tok, part)),
            lax.dynamic_slice(cotangent, (0, row * part), (tok, part)),
        ],
        axis=1,
    )
    both = lax.all_gather(both, "expert", axis=0, tiled=True)
    both = lax.all_gather(both, "dp", axis=0, tiled=False)
    all_x = jnp.transpose(both[:, :, :part], (1, 0, 2)).reshape(n_ex * tok, width)
    all_c = jnp.transpose(both[:, :, part:], (1, 0, 2)).reshape(n_ex * tok, width)
    gates = lax.all_to_all(table, "expert", split_axis=0, concat_axis=0, tiled=True)
    return weights, all_x, all_c, gates


def body(dense_weights, tokens, cotangent, routes, route_gates, unit_perm, slab_owner):
    n_dp = lax.axis_size("dp")
    n_ex = lax.axis_size("expert")
    row = lax.axis_index("dp")
    col = lax.axis_index("expert")
    _, block_units, feat = dense_weights.shape
    copies, total_units = unit_perm.shape
    slabs = n_ex // copies
    slab_units = total_units // slabs
    share = slab_units // n_dp
    pick = share // n_dp
    tok, width = tokens.shape

    shares = unit_perm.reshape(n_ex, n_dp, share)
    dest = jnp.transpose(shares[slab_owner], (1, 0, 2)).reshape(n_dp * n_ex, share)
    mask, rank = block_ranks(dest // block_units, row)
    place = jnp.where(mask, rank, -1)
    hit = place[:, None, :] == lax.broadcasted_iota(jnp.int32, (1, pick, 1), 1)
    units = jnp.sum(jnp.where(hit, (dest - row * block_units)[:, None, :], 0), axis=2)
    onehot = (
        units.reshape(-1, 1) == lax.broadcasted_iota(jnp.int32, (1, block_units), 1)
    ).astype(BF16)
    side = jnp.concatenate([dense_weights[0], dense_weights[1], dense_weights[2]], axis=1)
    picked = dot(onehot, side, 1, 0).astype(BF16)
    picked = picked.reshape(n_dp * n_ex, pick, 3 * feat)
    mine = lax.dynamic_slice(
        shares, (slab_owner[col], row, 0), (1, 1, share)
    ).reshape(1, share)
    mine_block = mine // block_units
    mask, rank = block_ranks(
        jnp.broadcast_to(mine_block, (n_dp, share)),
        lax.broadcasted_iota(jnp.int32, (n_dp, 1), 0),
    )
    at = jnp.sum(
        jnp.where(mask, rank + lax.broadcasted_iota(jnp.int32, (n_dp, 1), 0) * pick, 0), axis=0
    )
    order = (lax.broadcasted_iota(jnp.int32, (share, share), 1) == at[:, None]).astype(BF16)

    gate_table = jnp.sum(
        jnp.where(
            routes[None, :, :] == lax.broadcasted_iota(jnp.int32, (n_ex, 1, 1), 0),
            route_gates[None, :, :],
            0.0,
        ),
        axis=2,
    )
    if pick % 8 == 0 and feat % 128 == 0 and width // n_dp % 128 == 0:
        weights, all_x, all_c, gate = gather_all(
            n_dp, n_ex, picked, tokens, cotangent, gate_table
        )
    else:
        weights, all_x, all_c, gate = gather_plain(
            n_dp, n_ex, row, picked, tokens, cotangent, gate_table
        )
    w_gate, w_up, w_down = weights[0], weights[1], weights[2]
    gate = gate.reshape(n_ex * tok, 1)
    copy_id = slab_owner[col] // slabs
    owner_block = lax.broadcasted_iota(jnp.int32, (n_ex, tok), 0).reshape(n_ex * tok, 1)
    both_weight = gate + (owner_block * copies // n_ex == copy_id).astype(F32)

    pre_gate = dot(all_x, w_gate, 1, 1)
    pre_up = dot(all_x, w_up, 1, 1)
    d_hidden = dot(all_c, w_down, 1, 1)
    act, slope = silu_parts(pre_gate)
    hidden = act * pre_up
    d_gate = d_hidden * pre_up * slope
    d_up = d_hidden * act

    out = dot((both_weight * hidden).astype(BF16), w_down, 1, 0).astype(BF16)
    back = (
        dot((both_weight * d_gate).astype(BF16), w_gate, 1, 0)
        + dot((both_weight * d_up).astype(BF16), w_up, 1, 0)
    ).astype(BF16)

    acts = [(gate * values).astype(BF16) for values in (d_gate, d_up, hidden)]
    if out.size * out.dtype.itemsize <= 1 << 23:
        mixed, token_grad, weight_grads = halving_sum(
            n_dp, n_ex, [out, back], acts + [order], [all_x, all_c]
        )
    else:
        acts = [dot(order, values, 1, 1).astype(BF16) for values in acts]
        weight_grads = jnp.stack(
            [dot(acts[0], all_x, 1, 0), dot(acts[1], all_x, 1, 0), dot(acts[2], all_c, 1, 0)]
        ).astype(BF16)[None]
        (mixed,) = halving_sum(n_dp, n_ex, [out])
        (token_grad,) = halving_sum(n_dp, n_ex, [back])
    return (mixed, token_grad, weight_grads)


def solution(mesh):
    in_specs = (
        P(None, "dp", "expert"),
        P("expert", None),
        P("expert", None),
        P("expert", None),
        P("expert", None),
        P(),
        P(),
    )
    out_specs = (P("expert", "dp"), P("expert", "dp"), P("expert", None, "dp", None))
    return jax.shard_map(body, mesh=mesh, in_specs=in_specs, out_specs=out_specs, check_vma=False)
```

profile of v0, /device:TPU:0, one launch (start us, length us, event | category | flops | bytes accessed | tf_op | source)
XLA Modules:
  0.0 239.1 jit_solution(4637445084214802154)
XLA Ops:
  0.6 0.9 reshape.144
  1.5 0.7 compare_select_fusion
  2.2 0.6 gather_fusion
  2.8 0.1 fusion.40
  2.9 0.2 fusion.25
  3.1 0.6 select_reduce_fusion
  3.7 0.1 eq.79
  3.8 1.7 slice_bitcast_fusion.2
  5.5 0.0 copy-start.6
  5.5 0.0 copy-start.7
  5.5 9.4 %fusion.2 = bf16[2816,768]{1,0:T(8,128)(2,1)} fusion(s32[2816]{0:T(1024)S(1)} %eq.79, bf16[1408,256]{1,0:T(8,128)(2,1)S(1)} %get-tuple-element.16, bf16[1408,256]{1,0:T(8,128)(2,1)S(1)} %get-tuple-element.17, bf16[1408,256]{1,0:T(8,128)(2,1)S(1)} %get-tuple-element.15), kind=kOutput, calls=%fused_computation.5 | convolution fusion | flops 6102745088 | bytes 6499328 | tf_op jit(solution)/shard_map/dot_general | solution.py:20
  14.9 0.0 copy-done.6
  14.9 0.0 copy-done.7
  14.9 0.6 select_reduce_fusion.1
  15.5 122.2 %gather_all.1 = (bf16[3,352,2048]{2,1,0:T(8,128)(2,1)}, bf16[1024,2048]{1,0:T(8,128)(2,1)}, bf16[1024,2048]{1,0:T(8,128)(2,1)}, f32[8,1,128]{2,1,0:T(1,128)}) custom-call(bf16[32,88,768]{2,1,0:T(8,128)(2,1)} %bitcast.72, bf16[128,2048]{1,0:T(8,128)(2,1)} %tokens.1, bf16[128,2048]{1,0:T(8,128)(2,1)} %cotangent.1, f32[8,1,128]{2,1,0:T(1,128)} %bitcast.74), custom_call_target="tpu_custom_call" | custom-call | tf_op jit(solution)/shard_map/gather_all/pallas_call | solution.py:388
  137.7 0.0 copy-start.1
  137.7 0.0 copy-start.2
  137.7 5.1 %fusion.13 = f32[1024,352]{1,0:T(8,128)S(1)} fusion(bf16[1024,2048]{1,0:T(8,128)(2,1)} %get-tuple-element.8.refs_6_, bf16[3,352,2048]{2,1,0:T(8,128)(2,1)} %get-tuple-element.9), kind=kOutput, calls=%fused_computation.27 | convolution fusion | flops 1476395008 | bytes 7077888 | tf_op jit(solution)/shard_map/dot_general | solution.py:20
  142.8 0.0 copy-start.9
  142.8 0.0 copy-done.1
  142.9 0.0 copy-done.2
  142.9 0.0 copy-start
  142.9 0.0 copy-start.5
  142.9 2.3 fusion.9
  145.2 0.0 copy-start.3
  145.2 0.0 copy-done.9
  145.3 0.4 copy-done
  145.6 0.0 copy-done.5
  145.6 0.0 copy-start.8
  145.6 4.4 %multiply_convert_fusion.2 = (bf16[1024,352]{1,0:T(8,128)(2,1)}, f32[1024,352]{1,0:T(8,128)S(1)}, bf16[1024,352]{1,0:T(8,128)(2,1)}, bf16[1024,352]{1,0:T(8,128)(2,1)}, f32[1024,352]{1,0:T(8,128)S(1)}) fusion(f32[1024]{0:T(1024)S(1)} %bitcast.75, f32[1024,352]{1,0:T(8,128)S(1)} %fusion.9, f32[1024,352]{1,0:T(8,128)S(1)} %fusion.13, ...), kind=kOutput, calls=%fused_computation.16 | convolution fusion | flops 1482883072 | bytes 13832192 | tf_op jit(solution)/shard_map/dot_general | solution.py:20
  150.0 0.0 copy-done.3
  150.0 0.0 copy-done.8
  150.0 0.6 dynamic_slice.7
  153.2 0.0 copy-start.4
  153.2 3.9 %fusion.15 = f32[1024,2048]{1,0:T(8,128)S(1)} fusion(bf16[3,352,2048]{2,1,0:T(8,128)(2,1)} %get-tuple-element.9, f32[1024,352]{1,0:T(8,128)S(1)} %get-tuple-element.12, f32[1024]{0:T(1024)S(1)} %convert_add_fusion), kind=kOutput, calls=%fused_computation.29 | convolution fusion | flops 1477115904 | bytes 11276288 | tf_op jit(solution)/shard_map/dot_general | solution.py:20
  157.1 0.0 copy-done.4
  157.1 0.0 copy-start.10
  157.1 6.0 %add_convert_fusion.refs_1_ = bf16[1024,2048]{1,0:T(8,128)(2,1)} fusion(f32[1024,2048]{1,0:T(8,128)S(1)} %fusion.15, bf16[3,352,2048]{2,1,0:T(8,128)(2,1)} %get-tuple-element.9, f32[1024]{0:T(1024)S(1)} %convert_add_fusion, f32[1024,352]{1,0:T(8,128)S(1)} %copy-done.4, f32[1024,352]{1,0:T(8,128)S(1)} %get-tuple-element.20), kind=kOutput, calls=%fused_computation.3 | convolution fusion | flops 1483112448 | bytes 16912384 | tf_op jit(solution)/shard_map/dot_general | solution.py:20
  163.1 0.0 copy-done.10
  163.1 5.9 %convolution_convert_fusion.refs_0_ = bf16[1024,2048]{1,0:T(8,128)(2,1)} fusion(bf16[3,352,2048]{2,1,0:T(8,128)(2,1)} %get-tuple-element.9, f32[1024]{0:T(1024)S(1)} %convert_add_fusion, f32[1024,352]{1,0:T(8,128)S(1)} %copy-done.10, f32[1024,352]{1,0:T(8,128)S(1)} %get-tuple-element.20), kind=kOutput, calls=%fused_computation.8 | convolution fusion | flops 1481015296 | bytes 8523776 | tf_op jit(solution)/shard_map/dot_general | solution.py:20
  170.4 0.2 fusion.28
  170.6 0.8 fusion.34.refs_5_
  171.4 59.7 %halving_sum.1 = (bf16[128,512]{1,0:T(8,128)(2,1)}, bf16[128,512]{1,0:T(8,128)(2,1)}, bf16[1,3,352,2048]{3,2,1,0:T(8,128)(2,1)}) custom-call(bf16[1024,2048]{1,0:T(8,128)(2,1)} %convolution_convert_fusion.refs_0_, bf16[1024,2048]{1,0:T(8,128)(2,1)} %add_convert_fusion.refs_1_, bf16[1024,352]{1,0:T(8,128)(2,1)} %get-tuple-element.11.refs_2_, ...), custom_call_target="tpu_custom_call" | custom-call | tf_op jit(solution)/shard_map/halving_sum/pallas_call | solution.py:238
  231.0 1.6 copy.82
  232.6 1.6 copy.83
  234.2 4.9 %copy.84 = bf16[1,3,352,2048]{3,2,1,0:T(8,128)(2,1)} copy(bf16[1,3,352,2048]{3,2,1,0:T(8,128)(2,1)} %get-tuple-element.26) | data formatting | bytes 8650752
  (8 shorter events, 0.1 us)
Async XLA Ops:
  5.5 9.4 %copy-start.6 = (f32[128,4]{0,1:T(4,128)S(1)}, f32[128,4]{0,1:T(4,128)}, u32[]{:S(2)}) copy-start(f32[128,4]{0,1:T(4,128)} %param.11) | copy-start | bytes 6148
  5.5 9.4 %copy-start.7 = (s32[128,4]{0,1:T(4,128)S(1)}, s32[128,4]{0,1:T(4,128)}, u32[]{:S(2)}) copy-start(s32[128,4]{0,1:T(4,128)} %param.10) | copy-start | bytes 6148
  137.7 5.2 %copy-start.1 = (bf16[1024,2048]{1,0:T(8,128)(2,1)S(1)}, bf16[1024,2048]{1,0:T(8,128)(2,1)}, u32[]{:S(2)}) copy-start(bf16[1024,2048]{1,0:T(8,128)(2,1)} %get-tuple-element.10.refs_7_) | copy-start | bytes 12582916
  137.7 5.2 %copy-start.2 = (bf16[3,352,2048]{2,1,0:T(8,128)(2,1)S(1)}, bf16[3,352,2048]{2,1,0:T(8,128)(2,1)}, u32[]{:S(2)}) copy-start(bf16[3,352,2048]{2,1,0:T(8,128)(2,1)} %get-tuple-element.9) | copy-start | bytes 12976132
  142.8 2.4 %copy-start.9 = (f32[1024,352]{1,0:T(8,128)}, f32[1024,352]{1,0:T(8,128)S(1)}, u32[]{:S(2)}) copy-start(f32[1024,352]{1,0:T(8,128)S(1)} %fusion.13) | copy-start | bytes 4325380
  142.9 2.7 %copy-start = (bf16[1024,2048]{1,0:T(8,128)(2,1)S(1)}, bf16[1024,2048]{1,0:T(8,128)(2,1)}, u32[]{:S(2)}) copy-start(bf16[1024,2048]{1,0:T(8,128)(2,1)} %get-tuple-element.8.refs_6_) | copy-start | bytes 12582916
  142.9 2.7 %copy-start.5 = (f32[8,1,128]{2,1,0:T(1,128)S(1)}, f32[8,1,128]{2,1,0:T(1,128)}, u32[]{:S(2)}) copy-start(f32[8,1,128]{2,1,0:T(1,128)} %get-tuple-element.7) | copy-start | bytes 12292
  145.2 4.8 %copy-start.3 = (f32[1024,352]{1,0:T(8,128)}, f32[1024,352]{1,0:T(8,128)S(1)}, u32[]{:S(2)}) copy-start(f32[1024,352]{1,0:T(8,128)S(1)} %fusion.9) | copy-start | bytes 4325380
  145.6 4.4 %copy-start.8 = (s32[8]{0:T(128)S(1)}, s32[8]{0:T(128)}, u32[]{:S(2)}) copy-start(s32[8]{0:T(128)} %param.13) | copy-start | bytes 100
  153.2 3.9 %copy-start.4 = (f32[1024,352]{1,0:T(8,128)S(1)}, f32[1024,352]{1,0:T(8,128)}, u32[]{:S(2)}) copy-start(f32[1024,352]{1,0:T(8,128)} %copy-done.3) | copy-start | bytes 4325380
  157.1 6.0 %copy-start.10 = (f32[1024,352]{1,0:T(8,128)S(1)}, f32[1024,352]{1,0:T(8,128)}, u32[]{:S(2)}) copy-start(f32[1024,352]{1,0:T(8,128)} %copy-done.9) | copy-start | bytes 4325380
where the time goes:
time: 240 us; the launch traced here: 239 us
  Pallas kernels  182 us (76%)
  matrix products  37.3 us (16%)
  local copies, waits for them, and re-layouts  12.3 us (5%)
  between operations  4.74 us (2%)
  other arithmetic  2.91 us (1%)
    pallas_call x1, Pallas kernels, gather_all(): pl.pallas_call(functools.partial(gather_kernel, n_dp, n_ex), out_shape=[j...  122 us
    pallas_call x1, Pallas kernels, halving_sum(): pl.pallas_call(functools.partial(halving_kernel, n_dp, n_ex, n_arrays, bo...  59.7 us
    dot_general x7, matrix products, dot(): lax.dot_general(left, right, (((left_dim,), (right_dim,)), ((), ())), pre...  37 us
    unnamed x25, local copies, waits for them, and re-layouts  8.47 us

commit v1 on v0

--- a/solution.py
+++ b/solution.py
@@ -257,156 +257,537 @@
     return index
 
 
-def gather_kernel(
-    n_dp, n_ex, picked, tokens, cotangent, table, weights, all_x, all_c, gates, load_sem, row_sem, tok_send, tok_recv
-):
+def fused_kernel(n_dp, n_ex, *refs):
+    shares, owner, table, dense, tokens, cotangent, mixed, token_grad, grads, *refs = refs
+    side, full, picked, weights, pre, mult, own_acts, far_acts, *refs = refs
+    data, recv, swap, upper, order_ref, act_rows, grad_rows, gates, gate_col, both_col, *refs = refs
+    load_sem, gate_sem, row_send, row_recv, fwd_send, fwd_recv, tok_send, tok_recv, *refs = refs
+    act_sem, halve_send, halve_recv, swap_sem, out_sem = refs
+
     row, col = lax.axis_index("dp"), lax.axis_index("expert")
     me = row * n_ex + col
-    blocks, pick, wide = picked.shape
-    feat = wide // 3
-    tok, width = tokens.shape
-    part = width // n_dp
+    core, spot_x = row % 2, row // 2
+    n_x = n_dp // 2
+    chip = spot_x * n_ex + col
+    block_units, feat = side.shape[1:]
+    pick, share = picked.shape[2], shares.shape[2]
+    padded = weights.shape[1] // (2 * n_dp)
+    half_units = n_dp * padded
+    width = full.shape[2]
+    tok = tokens.shape[0]
+    quarter = tok // n_dp
+    half = full.shape[1] // 2
     dp_bits, ex_bits = log2(n_dp), log2(n_ex)
+    bits = dp_bits + ex_bits
+    sibling = peer(flip(me, ex_bits), n_ex)
+    mesh_id = pl.DeviceIdType.MESH
+
+    def remote(src, dst, send_sem, recv_sem, device):
+        return pltpu.make_async_remote_copy(
+            src_ref=src,
+            dst_ref=dst,
+            send_sem=send_sem,
+            recv_sem=recv_sem,
+            device_id=device,
+            device_id_type=mesh_id,
+        )
+
+    def wait(view, sem):
+        pltpu.make_async_copy(view, view, sem).wait()
+
+    def place(at, device):
+        where = device // n_ex
+        start = where % 2 * half + where // 2 * (n_ex * quarter) + device % n_ex * quarter
+        return full.at[at, pl.ds(pl.multiple_of(start, quarter), quarter), :]
+
+    for at, source in enumerate((tokens, cotangent)):
+        pltpu.make_async_copy(
+            source.at[pl.ds(pl.multiple_of(row * quarter, quarter), quarter), :],
+            place(at, me),
+            load_sem.at[at],
+        ).start()
+    pltpu.make_async_copy(dense, side, load_sem.at[2]).start()
+    pltpu.make_async_copy(table.at[col], gates.at[col], gate_sem.at[1]).start()
+
+    if padded > pick:
+        for k in range(3):
+            for slot in range(2 * n_dp):
+                rows = pl.ds(slot * padded + pick, padded - pick)
+                weights[k, rows, :] = jnp.zeros((padded - pick, width), BF16)
+
+    barrier = pltpu.get_barrier_semaphore()
+    for mask in range(1, n_dp * n_ex):
+        pl.semaphore_signal(
+            barrier, inc=1, device_id=peer(flip_mask(me, mask), n_ex), device_id_type=mesh_id
+        )
+    upper[...] = (
+        lax.broadcasted_iota(jnp.int32, (share, share), 0)
+        < lax.broadcasted_iota(jnp.int32, (share, share), 1)
+    ).astype(BF16)
+    pl.semaphore_wait(barrier, n_dp * n_ex - 1)
+
+    for at in range(2):
+        wait(place(at, me), load_sem.at[at])
+
     ex_order = list(range(ex_bits - 1, -1, -1))
     dp_order = [ex_bits + bit for bit in range(dp_bits - 1, -1, -1)]
-    orders = [ex_order + dp_order, ex_order + dp_order]
-    if dp_bits > 1:
-        orders[1] = ex_order[:-1] + [dp_order[0], ex_order[-1]] + dp_order[1:]
-    fulls = (all_x, all_c)
-
-    def place(full, device):
-        return full.at[
-            pl.ds(pl.multiple_of(device % n_ex * tok, tok), tok),
-            pl.ds(pl.multiple_of(device // n_ex * part, part), part),
-        ]
-
-    for at, (source, full) in enumerate(((tokens, all_x), (cotangent, all_c))):
-        pltpu.make_async_copy(
-            source.at[:, pl.ds(pl.multiple_of(row * part, part), part)], place(full, me), load_sem.at[at]
-        ).start()
-
-    def spot(k):
-        return weights.at[
-            k,
-            pl.ds(pl.multiple_of(row * pick, 8), pick),
-            pl.ds(pl.multiple_of(col * feat, feat), feat),
-        ]
-
-    for k in range(3):
-        pltpu.make_async_copy(
-            picked.at[me, :, pl.ds(k * feat, feat)], spot(k), row_sem.at[1]
-        ).start()
-    pltpu.make_async_copy(table.at[col], gates.at[col], row_sem.at[3]).start()
-
-    barrier = pltpu.get_barrier_semaphore()
-    for mask in range(1, blocks):
-        pl.semaphore_signal(
-            barrier,
-            inc=1,
-            device_id=peer(flip_mask(me, mask), n_ex),
-            device_id_type=pl.DeviceIdType.MESH,
-        )
-    pl.semaphore_wait(barrier, blocks - 1)
-    for at, full in enumerate(fulls):
-        pltpu.make_async_copy(place(full, me), place(full, me), load_sem.at[at]).wait()
-
-    def send_tokens(at, step):
-        full, order = fulls[at], orders[at]
-
-        def one(choice, carry):
-            device = me
-            for bit, other in enumerate(order[:step]):
-                mine = me // (1 << other) % 2
-                device = device + (choice // (1 << bit) % 2 - mine) * (1 << other)
-            pltpu.make_async_remote_copy(
-                src_ref=place(full, device),
-                dst_ref=place(full, device),
-                send_sem=tok_send.at[at, step],
-                recv_sem=tok_recv.at[at, step],
-                device_id=peer(flip(me, order[step]), n_ex),
-                device_id_type=pl.DeviceIdType.MESH,
-            ).start()
-            return carry
-
-        lax.fori_loop(0, 1 << step, one, 0)
-
-    def wait_tokens(at, step, sem):
-        rows = min(1 << step, n_ex)
-        view = fulls[at].at[pl.ds(0, rows * tok), pl.ds(0, (1 << step) // rows * part)]
-        pltpu.make_async_copy(view, view, sem.at[at, step]).wait()
-
-    def send_rows(mask):
-        device = flip_mask(me, mask)
-        for k in range(3):
-            pltpu.make_async_remote_copy(
-                src_ref=picked.at[device, :, pl.ds(k * feat, feat)],
-                dst_ref=spot(k),
-                send_sem=row_sem.at[0],
-                recv_sem=row_sem.at[1],
-                device_id=peer(device, n_ex),
-                device_id_type=pl.DeviceIdType.MESH,
-            ).start()
-
-    steps = dp_bits + ex_bits
-    masks = [at * 11 % blocks for at in range(1, blocks)]
-    chunk = -(-len(masks) // steps)
+    tok_orders = [
+        ex_order + dp_order,
+        ex_order[:-1] + [dp_order[0], ex_order[-1]] + dp_order[1:],
+    ]
+
+    def send_tokens(step):
+        for at in range(2):
+            order = tok_orders[at]
+
+            def one(choice, carry, at=at, order=order):
+                device = me
+                for bit, other in enumerate(order[:step]):
+                    mine = me // (1 << other) % 2
+                    device = device + (choice // (1 << bit) % 2 - mine) * (1 << other)
+                remote(
+                    place(at, device),
+                    place(at, device),
+                    tok_send.at[at, step],
+                    tok_recv.at[at, step],
+                    peer(flip(me, order[step]), n_ex),
+                ).start()
+                return carry
+
+            lax.fori_loop(0, 1 << step, one, 0)
+
+    def wait_tokens(step, sem):
+        for at in range(2):
+            wait(full.at[at, pl.ds(0, (1 << step) * quarter), :], sem.at[at, step])
+
+    send_tokens(0)
     for mask in range(1, n_ex):
         device = flip_mask(me, mask)
-        pltpu.make_async_remote_copy(
-            src_ref=table.at[device % n_ex],
-            dst_ref=gates.at[col],
-            send_sem=row_sem.at[2],
-            recv_sem=row_sem.at[3],
-            device_id=peer(device, n_ex),
-            device_id_type=pl.DeviceIdType.MESH,
+        remote(
+            table.at[device % n_ex],
+            gates.at[col],
+            gate_sem.at[0],
+            gate_sem.at[1],
+            peer(device, n_ex),
         ).start()
-    for step in range(steps):
-        for at in range(2):
-            if step:
-                wait_tokens(at, step - 1, tok_recv)
-            send_tokens(at, step)
-        for mask in masks[step * chunk : (step + 1) * chunk]:
+    wait(side, load_sem.at[2])
+
+    def ranks(mask):
+        return jnp.dot(mask.astype(BF16), upper[...], preferred_element_type=F32)
+
+    def send_rows(mask):
+        target = flip_mask(col, mask)
+        local = shares[owner[target]] - row * block_units
+        inside = jnp.logical_and(local >= 0, local < block_units)
+        spots = jnp.where(inside, ranks(inside), -1.0)
+        values = (local + 1).astype(F32)
+        hots = []
+        for g in range(n_dp):
+            hit = spots[g : g + 1, :] == lax.broadcasted_iota(
+                jnp.int32, (padded, share), 0
+            ).astype(F32)
+            units = jnp.sum(jnp.where(hit, values[g : g + 1, :], 0.0), axis=1, keepdims=True)
+            hots.append(
+                (
+                    units.astype(jnp.int32) - 1
+                    == lax.broadcasted_iota(jnp.int32, (padded, block_units), 1)
+                ).astype(BF16)
+            )
+        hot = jnp.concatenate(hots, axis=0)
+        for k in range(3):
+            rows = jnp.dot(hot, side[k], preferred_element_type=F32).astype(BF16)
+            for g in range(n_dp):
+                picked[mask * n_dp + g, k] = rows[g * padded : g * padded + pick, :]
+        for turn in range(n_dp):
+            g = flip_mask(row, turn)
+
+            def one(k, carry, g=g, turn=turn):
+                source = picked.at[mask * n_dp + g, k]
+                start = pl.multiple_of((g % 2 * n_dp + row) * padded, padded)
+                target_ref = weights.at[
+                    k,
+                    pl.ds(start, pick),
+                    pl.ds(pl.multiple_of(col * feat, feat), feat),
+                ]
+                if mask == 0 and turn == 0:
+                    pltpu.make_async_copy(source, target_ref, row_recv.at[col]).start()
+                else:
+                    remote(
+                        source,
+                        target_ref,
+                        row_send.at[0],
+                        row_recv.at[col],
+                        {"dp": g, "expert": target},
+                    ).start()
+                return carry
+
+            lax.fori_loop(0, 3, one, 0)
+
+    far, near = [m for m in range(n_ex) if m >= n_ex // 2], [m for m in range(1, n_ex // 2)] + [0]
+    masks = [m for pair in zip(far, near) for m in pair]
+    per_step = 2
+    for step in range(bits - 1):
+        for mask in masks[step * per_step : (step + 1) * per_step]:
             send_rows(mask)
-
-    for at in range(2):
-        wait_tokens(at, steps - 1, tok_recv)
-        for step in range(steps):
-            wait_tokens(at, step, tok_send)
-    sent = picked.at[pl.ds(0, blocks - 1)]
-    pltpu.make_async_copy(sent, sent, row_sem.at[0]).wait()
-    pltpu.make_async_copy(weights, weights, row_sem.at[1]).wait()
-    sent = table.at[pl.ds(0, n_ex - 1)]
-    pltpu.make_async_copy(sent, sent, row_sem.at[2]).wait()
-    pltpu.make_async_copy(gates, gates, row_sem.at[3]).wait()
-
-
-def gather_all(n_dp, n_ex, picked, tokens, cotangent, table):
-    blocks, pick, wide = picked.shape
+        wait_tokens(step, tok_recv)
+        send_tokens(step + 1)
+    for mask in masks[(bits - 1) * per_step :]:
+        send_rows(mask)
+
+    mine = shares[owner[col], pl.ds(row, 1), :]
+    at_row = jnp.zeros((1, share), F32)
+    for b in range(n_dp):
+        inside = jnp.logical_and(mine >= b * block_units, mine < (b + 1) * block_units)
+        at_row = at_row + jnp.where(inside, ranks(inside) + float(b * padded), 0.0)
+    diagonal = lax.broadcasted_iota(jnp.int32, (share, share), 0) == lax.broadcasted_iota(
+        jnp.int32, (share, share), 1
+    )
+    at_col = jnp.sum(jnp.where(diagonal, at_row, 0.0), axis=1, keepdims=True)
+    order_ref[...] = (
+        at_col.astype(jnp.int32) == lax.broadcasted_iota(jnp.int32, (share, half_units), 1)
+    ).astype(BF16)
+
+    wait(table.at[pl.ds(0, n_ex - 1)], gate_sem.at[0])
+    wait(gates, gate_sem.at[1])
+    copy_id = owner[col] // (n_ex // 2)
+    lanes = lax.broadcasted_iota(jnp.int32, (quarter, tok), 1)
+    below = lax.broadcasted_iota(jnp.int32, (quarter, tok), 0)
+    for xq in range(n_x):
+
+        def column(block, carry, xq=xq):
+            hit = lanes == below + (xq * 2 + core) * quarter
+            value = jnp.sum(jnp.where(hit, gates[block], 0.0), axis=1, keepdims=True)
+            value = jnp.broadcast_to(value, (quarter, 128))
+            blocks = jnp.full((quarter, 128), block * 2 // n_ex, jnp.int32)
+            rows = pl.ds(pl.multiple_of((xq * n_ex + block) * quarter, quarter), quarter)
+            gate_col[rows, :] = value
+            both_col[rows, :] = value + (blocks == copy_id).astype(F32)
+            return carry
+
+        lax.fori_loop(0, n_ex, column, 0)
+
+    my_rows = pl.ds(pl.multiple_of(core * half, half), half)
+    my_units = pl.ds(pl.multiple_of(core * half_units, half_units), half_units)
+    far_units = pl.ds(pl.multiple_of((1 - core) * half_units, half_units), half_units)
+    n_tile = min(256, 2 * half_units)
+    tiles = 2 * half_units // n_tile
+
+    def columns(mask):
+        return pl.ds(pl.multiple_of(flip_mask(col, mask) * feat, feat), feat)
+
+    def forward(mask):
+        f = flip_mask(col, mask)
+        count = n_dp * pick
+        wait(weights.at[:, pl.ds(0, count), columns(mask)], row_recv.at[f])
+        for k in range(3):
+            view = weights.at[k, my_units, columns(mask)]
+            remote(view, view, fwd_send.at[0], fwd_recv.at[f], sibling).start()
+
+    def accumulate(mask, first):
+        f = flip_mask(col, mask)
+        wait(weights.at[:, far_units, columns(mask)], fwd_recv.at[f])
+
+        def one(index, carry):
+            k, n = index // tiles, index % tiles
+            units = pl.ds(pl.multiple_of(n * n_tile, n_tile), n_tile)
+            value = dot(full[k // 2, my_rows, columns(mask)], weights[k, units, columns(mask)], 1, 1)
+            if first:
+                pre[k, :, units] = value
+            else:
+                pre[k, :, units] = pre[k, :, units] + value
+            return carry
+
+        lax.fori_loop(0, 3 * tiles, one, 0)
+
+    for at, mask in enumerate(masks):
+        forward(mask)
+        if at:
+            accumulate(masks[at - 1], at == 1)
+    accumulate(masks[-1], False)
+
+    r_tile = 32
+
+    def activate(share_at, keep):
+        units = pl.ds(pl.multiple_of(share_at * half_units, half_units), half_units)
+
+        def one(index, carry):
+            rows = pl.ds(pl.multiple_of(index * r_tile, r_tile), r_tile)
+            reps = (1, half_units // 128)
+            gate = jnp.tile(gate_col[rows, :], reps)
+            both = jnp.tile(both_col[rows, :], reps)
+            act, slope = silu_parts(pre[0, rows, units])
+            up, d_hidden = pre[1, rows, units], pre[2, rows, units]
+            values = (d_hidden * up * slope, d_hidden * act, act * up)
+            for k, value in enumerate(values):
+                mult[k, rows, units] = (both * value).astype(BF16)
+                if keep:
+                    own_acts[core, k, rows, :] = (gate * value).astype(BF16)
+                else:
+                    far_acts[k, rows, :] = (gate * value).astype(BF16)
+            return carry
+
+        lax.fori_loop(0, half // r_tile, one, 0)
+
+    activate(1 - core, False)
+    act_copy = remote(far_acts, own_acts.at[core], act_sem.at[0], act_sem.at[1], sibling)
+    act_copy.start()
+    activate(core, True)
+
+    chip_bits = bits - 1
+    x_place, y_place, z_low = chip_bits - 1, 0, 1
+    rest = list(range(2, chip_bits - 1))
+    classes = {
+        "a": [x_place, y_place, z_low] + rest,
+        "b": [y_place, z_low, x_place] + rest,
+        "c": [z_low, x_place, y_place] + rest,
+    }
+    kinds = ["a", "a", "a", "c", "b", "b", "b", "c"]
+    turns = [0, 4, 3, 1, 5, 7, 2, 6]
+    chunk = data.shape[3]
+    per_array = width // n_x // chunk
+    r_rows = data.shape[2]
+
+    def chip_peer(place_at):
+        if place_at == x_place:
+            return peer(flip(me, bits - 1), n_ex)
+        return peer(flip(me, place_at), n_ex)
+
+    def block_of(stream, step, choice, sent):
+        order = classes[kinds[stream]]
+        index = 0
+        for place_at in order[: step + 1]:
+            index = index + chip // (1 << place_at) % 2 * (1 << place_at)
+        if sent:
+            index = flip(index, order[step])
+        for bit, place_at in enumerate(sorted(order[step + 1 :])):
+            index = index + choice // (1 << bit) % 2 * (1 << place_at)
+        return index
+
+    def count(step):
+        return 1 << (chip_bits - 1 - step)
+
+    def offset(step):
+        return (1 << chip_bits) - (1 << (chip_bits - step))
+
+    def send(stream, step, choice):
+        remote(
+            data.at[stream, block_of(stream, step, choice, True)],
+            recv.at[stream, offset(step) + choice],
+            halve_send.at[stream, step],
+            halve_recv.at[stream, step],
+            chip_peer(classes[kinds[stream]][step]),
+        ).start()
+
+    def region(stream, step):
+        return recv.at[stream, pl.ds(offset(step), count(step))]
+
+    def number(stream, step, choice, sent):
+        order = classes[kinds[stream]]
+        later = sorted(order[step + 1 :])
+        place_at = order[step + 1]
+        mine_bit = chip // (1 << place_at) % 2
+        value = (1 - mine_bit if sent else mine_bit) * (1 << later.index(place_at))
+        for bit, other in enumerate(sorted(order[step + 2 :])):
+            value = value + choice // (1 << bit) % 2 * (1 << later.index(other))
+        return value
+
+    def product(stream, xq):
+        array, j = stream // per_array, stream % per_array
+        cols = pl.ds(pl.multiple_of(xq * (width // n_x) + j * chunk, chunk), chunk)
+        if array == 0:
+            value = jnp.dot(mult[2], weights[2, :, cols], preferred_element_type=F32)
+        else:
+            value = jnp.dot(mult[0], weights[0, :, cols], preferred_element_type=F32)
+            value = value + jnp.dot(mult[1], weights[1, :, cols], preferred_element_type=F32)
+        value = value.astype(BF16).reshape(n_x, n_ex, quarter, chunk)
+        for part in range(n_x):
+            data[
+                stream,
+                pl.ds(pl.multiple_of(xq * n_ex, n_ex), n_ex),
+                part * quarter : (part + 1) * quarter,
+                :,
+            ] = value[part]
+
+    def begin(stream):
+        def first(choice, carry):
+            send(stream, 0, choice)
+            return carry
+
+        lax.fori_loop(0, count(0), first, 0)
+
+    for stream in turns:
+        if kinds[stream] == "a":
+            product(stream, 1 - spot_x)
+            begin(stream)
+        else:
+
+            def both_sides(side_at, carry, stream=stream):
+                product(stream, side_at)
+                return carry
+
+            lax.fori_loop(0, n_x, both_sides, 0)
+            begin(stream)
+    for stream in turns:
+        if kinds[stream] == "a":
+            product(stream, spot_x)
+
+    def weight_grad(k):
+        for part in range(2):
+            act_rows[:, part * half : (part + 1) * half] = dot(
+                order_ref[...], own_acts[part, k], 1, 1
+            ).astype(BF16)
+        piece = min(512, width)
+
+        def one(step, carry):
+            where = pl.ds(pl.multiple_of(step * piece, piece), piece)
+            grad_rows[k, :, where] = jnp.dot(
+                act_rows[...], full[k // 2, :, where], preferred_element_type=F32
+            ).astype(BF16)
+            return carry
+
+        lax.fori_loop(0, width // piece, one, 0)
+        pltpu.make_async_copy(grad_rows.at[k], grads.at[0, k], out_sem.at[k]).start()
+
+    def combine(stream, step):
+        wait(region(stream, step), halve_recv.at[stream, step])
+        for sent in (True, False):
+
+            def add(choice, carry, sent=sent):
+                block = block_of(stream, step + 1, choice, sent)
+                slot = offset(step) + number(stream, step, choice, sent)
+                total = data[stream, block].astype(F32) + recv[stream, slot].astype(F32)
+                data[stream, block] = total.astype(BF16)
+                if sent:
+                    send(stream, step + 1, choice)
+                return carry
+
+            lax.fori_loop(0, count(step + 1), add, 0)
+
+    wait_tokens(bits - 1, tok_recv)
+    act_copy.wait()
+    fill = {(0, 0): 0, (0, 3): 1, (0, 6): 2}
+    for step in range(chip_bits - 1):
+        for at, stream in enumerate(turns):
+            if (step, at) in fill:
+                weight_grad(fill[step, at])
+            combine(stream, step)
+
+    last = chip_bits - 1
+    results = (mixed, token_grad)
+
+    def finish(array, i, keep):
+        owner_core = core if keep else 1 - core
+        stream = array * per_array + owner_core * (per_array // 2) + i
+        wait(recv.at[stream, pl.ds(offset(last), 1)], halve_recv.at[stream, last])
+        total = (
+            data[stream, chip].astype(F32) + recv[stream, offset(last)].astype(F32)
+        ).astype(BF16)
+        if keep:
+            put(array, i, core, total)
+        else:
+            data[stream, chip] = total
+            remote(
+                data.at[stream, chip],
+                swap.at[array, i],
+                swap_sem.at[0],
+                swap_sem.at[1],
+                sibling,
+            ).start()
+
+    def put(array, i, which, total):
+        for part in range(n_x):
+            start = pl.multiple_of((part * 2 + which) * quarter, quarter)
+            results[array][pl.ds(start, quarter), i * chunk : (i + 1) * chunk] = total[
+                part * quarter : (part + 1) * quarter
+            ]
+
+    for keep in (False, True):
+        for array in range(2):
+            for i in range(per_array // 2):
+                finish(array, i, keep)
+    wait(swap, swap_sem.at[1])
+    for array in range(2):
+        for i in range(per_array // 2):
+            put(array, i, 1 - core, swap[array, i])
+
+    for k in range(3):
+        pltpu.make_async_copy(grad_rows.at[k], grads.at[0, k], out_sem.at[k]).wait()
+    wait(picked.at[pl.ds(0, n_dp * n_ex - 1)], row_send.at[0])
+    wait(weights.at[:, my_units, :], fwd_send.at[0])
+    for step in range(bits):
+        wait_tokens(step, tok_send)
+    for step in range(chip_bits):
+        for stream in range(len(kinds)):
+            wait(region(stream, step), halve_send.at[stream, step])
+    wait(swap, swap_sem.at[0])
+
+
+def fused_step(n_dp, n_ex, shares, slab_owner, table, dense_weights, tokens, cotangent):
+    _, block_units, feat = dense_weights.shape
     tok, width = tokens.shape
-    steps = log2(blocks)
-    table = table.reshape(n_ex, 1, tok)
+    share = shares.shape[2]
+    pick = share // n_dp
+    padded = -(-pick // 16) * 16
+    half_units, half = n_dp * padded, n_ex * tok // 2
+    blocks, bits, n_x = n_dp * n_ex, log2(n_dp * n_ex), n_dp // 2
+    chips, chunk = blocks // 2, 256
+    streams = 2 * (width // n_x // chunk)
+    any_spec, vmem_spec = pl.BlockSpec(memory_space=pl.ANY), pl.BlockSpec(memory_space=pltpu.VMEM)
+    r_rows = tok // 2
     return pl.pallas_call(
-        functools.partial(gather_kernel, n_dp, n_ex),
+        functools.partial(fused_kernel, n_dp, n_ex),
         out_shape=[
-            jax.ShapeDtypeStruct((3, n_dp * pick, width), BF16),
-            jax.ShapeDtypeStruct((n_ex * tok, width), BF16),
-            jax.ShapeDtypeStruct((n_ex * tok, width), BF16),
-            jax.ShapeDtypeStruct((n_ex, 1, tok), F32),
+            jax.ShapeDtypeStruct((tok, width // n_dp), BF16),
+            jax.ShapeDtypeStruct((tok, width // n_dp), BF16),
+            jax.ShapeDtypeStruct((1, 3, share, width), BF16),
         ],
-        in_specs=[pl.BlockSpec(memory_space=pltpu.VMEM)] * 4,
-        out_specs=[pl.BlockSpec(memory_space=pl.ANY)] * 3
-        + [pl.BlockSpec(memory_space=pltpu.VMEM)],
+        in_specs=[
+            vmem_spec,
+            pl.BlockSpec(memory_space=pltpu.SMEM),
+            vmem_spec,
+            any_spec,
+            any_spec,
+            any_spec,
+        ],
+        out_specs=[vmem_spec, vmem_spec, any_spec],
         scratch_shapes=[
+            pltpu.VMEM((3, block_units, feat), BF16),
+            pltpu.VMEM((2, n_ex * tok, width), BF16),
+            pltpu.VMEM((blocks, 3, pick, feat), BF16),
+            pltpu.VMEM((3, 2 * half_units, width), BF16),
+            pltpu.VMEM((3, half, 2 * half_units), F32),
+            pltpu.VMEM((3, half, 2 * half_units), BF16),
+            pltpu.VMEM((2, 3, half, half_units), BF16),
+            pltpu.VMEM((3, half, half_units), BF16),
+            pltpu.VMEM((streams, chips, r_rows, chunk), BF16),
+            pltpu.VMEM((streams, chips - 1, r_rows, chunk), BF16),
+            pltpu.VMEM((2, streams // 4, r_rows, chunk), BF16),
+            pltpu.VMEM((share, share), BF16),
+            pltpu.VMEM((share, half_units), BF16),
+            pltpu.VMEM((share, n_ex * tok), BF16),
+            pltpu.VMEM((3, share, width), BF16),
+            pltpu.VMEM((n_ex, 1, tok), F32),
+            pltpu.VMEM((half, 128), F32),
+            pltpu.VMEM((half, 128), F32),
+            pltpu.SemaphoreType.DMA((3,)),
             pltpu.SemaphoreType.DMA((2,)),
-            pltpu.SemaphoreType.DMA((4,)),
-            pltpu.SemaphoreType.DMA((2, steps)),
-            pltpu.SemaphoreType.DMA((2, steps)),
+            pltpu.SemaphoreType.DMA((1,)),
+            pltpu.SemaphoreType.DMA((n_ex,)),
+            pltpu.SemaphoreType.DMA((1,)),
+            pltpu.SemaphoreType.DMA((n_ex,)),
+            pltpu.SemaphoreType.DMA((2, bits)),
+            pltpu.SemaphoreType.DMA((2, bits)),
+            pltpu.SemaphoreType.DMA((2,)),
+            pltpu.SemaphoreType.DMA((streams, bits - 1)),
+            pltpu.SemaphoreType.DMA((streams, bits - 1)),
+            pltpu.SemaphoreType.DMA((2,)),
+            pltpu.SemaphoreType.DMA((3,)),
         ],
         compiler_params=pltpu.CompilerParams(
-            collective_id=2, has_side_effects=True, vmem_limit_bytes=60 << 20
+            collective_id=2, has_side_effects=True, vmem_limit_bytes=63 << 20
         ),
-        name="gather_all",
-    )(picked, tokens, cotangent, table)
+        name="fused_step",
+    )(shares, slab_owner, table.reshape(n_ex, 1, tok), dense_weights, tokens, cotangent)
 
 
 def gather_plain(n_dp, n_ex, row, picked, tokens, cotangent, table):
@@ -445,6 +826,31 @@
     tok, width = tokens.shape
 
     shares = unit_perm.reshape(n_ex, n_dp, share)
+    gate_table = jnp.sum(
+        jnp.where(
+            routes[None, :, :] == lax.broadcasted_iota(jnp.int32, (n_ex, 1, 1), 0),
+            route_gates[None, :, :],
+            0.0,
+        ),
+        axis=2,
+    )
+    padded = -(-pick // 16) * 16
+    if (
+        copies == 2
+        and pick % 8 == 0
+        and feat % 256 == 0
+        and n_dp * padded % 128 == 0
+        and 2 * n_dp * padded % 256 == 0
+        and n_dp == 4
+        and n_ex == 8
+        and width == n_dp * 512
+        and tok == 128
+    ):
+        return tuple(
+            fused_step(
+                n_dp, n_ex, shares, slab_owner, gate_table, dense_weights, tokens, cotangent
+            )
+        )
     dest = jnp.transpose(shares[slab_owner], (1, 0, 2)).reshape(n_dp * n_ex, share)
     mask, rank = block_ranks(dest // block_units, row)
     place = jnp.where(mask, rank, -1)
@@ -469,22 +875,9 @@
     )
     order = (lax.broadcasted_iota(jnp.int32, (share, share), 1) == at[:, None]).astype(BF16)
 
-    gate_table = jnp.sum(
-        jnp.where(
-            routes[None, :, :] == lax.broadcasted_iota(jnp.int32, (n_ex, 1, 1), 0),
-            route_gates[None, :, :],
-            0.0,
-        ),
-        axis=2,
+    weights, all_x, all_c, gate = gather_plain(
+        n_dp, n_ex, row, picked, tokens, cotangent, gate_table
     )
-    if pick % 8 == 0 and feat % 128 == 0 and width // n_dp % 128 == 0:
-        weights, all_x, all_c, gate = gather_all(
-            n_dp, n_ex, picked, tokens, cotangent, gate_table
-        )
-    else:
-        weights, all_x, all_c, gate = gather_plain(
-            n_dp, n_ex, row, picked, tokens, cotangent, gate_table
-        )
     w_gate, w_up, w_down = weights[0], weights[1], weights[2]
     gate = gate.reshape(n_ex * tok, 1)
     copy_id = slab_owner[col] // slabs

time: 240 us -> 197 us (0.82)
  matrix products: 37.3 us -> 0 us
  between operations: 4.74 us -> 0.64 us
  Pallas kernels: 182 us -> 185 us
  local copies, waits for them, and re-layouts: 12.3 us -> 9.57 us
    dot_general x9 -> x0, matrix products: 37.3 us -> none  [the longest x7 37 us: dot(): lax.dot_general(left, right, (((left_dim,), (right_dim,)), ((), ())), pre...]
    pallas_call x2 -> x1, Pallas kernels: 182 us -> 185 us  [fused_step(): pl.pallas_call(functools.partial(fused_kernel, n_dp, n_ex), out_shape=[ja...]
    unnamed x25 -> x3, local copies, waits for them, and re-layouts: 8.47 us -> 8.04 us
where the time goes in v1:
time: 197 us
  Pallas kernels  185 us (94%)
  local copies, waits for them, and re-layouts  9.57 us (5%)
    pallas_call x1, Pallas kernels, fused_step(): pl.pallas_call(functools.partial(fused_kernel, n_dp, n_ex), out_shape=[ja...  185 us
    unnamed x3, local copies, waits for them, and re-layouts  8.04 us

profile of v1, /device:TPU:0, one launch (start us, length us, event | category | flops | bytes accessed | tf_op | source)
XLA Modules:
  0.0 196.8 jit_solution(2234947527009013662)
XLA Ops:
  0.6 1.3 select_reduce_fusion
  1.9 1.5 reshape.14.refs_0_
  3.5 185.3 %fused_step.1 = (bf16[128,512]{1,0:T(8,128)(2,1)}, bf16[128,512]{1,0:T(8,128)(2,1)}, bf16[1,3,352,2048]{3,2,1,0:T(8,128)(2,1)}) custom-call(s32[8,4,352]{2,1,0:T(4,128)} %reshape.14.refs_0_, s32[8]{0:T(128)} %refs_1_.1, f32[8,1,128]{2,1,0:T(1,128)} %bitcast.1, bf16[3,1408,256]{2,1,0:T(8,128)(2,1)} %refs_3_.1, bf16[128,2048]{1,0:T(8,128)(2,1)} %refs_4_.1, ...), custom_call_target="tpu_custom_call" | custom-call | tf_op jit(solution)/shard_map/fused_step/pallas_call | solution.py:737
  188.8 1.6 copy.15
  190.4 1.6 copy.16
  191.9 4.9 %copy.17 = bf16[1,3,352,2048]{3,2,1,0:T(8,128)(2,1)} copy(bf16[1,3,352,2048]{3,2,1,0:T(8,128)(2,1)} %get-tuple-element.8) | data formatting | bytes 8650752

commit v2 on v1

--- a/solution.py
+++ b/solution.py
@@ -257,12 +257,43 @@
     return index
 
 
+def gather_plan():
+    every = (3, 2, 1, 0)
+
+    def pick(*masks):
+        return [("pick", mask) for mask in masks]
+
+    def send(mask, *turns):
+        return [("send", mask, turn) for turn in turns]
+
+    def relay(mask, *turns):
+        return [("pass", mask, turn) for turn in turns]
+
+    def shared(*masks):
+        return [("share", mask) for mask in masks]
+
+    plan = pick(5) + send(5, 3, 2) + pick(1) + send(1, *every) + pick(0) + send(0, *every)
+    plan += send(5, 1, 0) + [("tokens", 1)]
+    plan += pick(4) + send(4, 3, 2, 1) + pick(3) + send(3, *every) + relay(5, 3, 2)
+    plan += [("tokens", 2)]
+    plan += pick(7) + send(7, 3, 2) + pick(2) + send(2, *every) + relay(5, 1, 0)
+    plan += [("tokens", 3)]
+    plan += relay(3, *every) + pick(6) + send(4, 0) + send(6, 3, 2) + send(7, 1)
+    plan += send(6, 1) + send(7, 0) + send(6, 0)
+    plan += relay(4, 3, 2, 1) + relay(2, 3, 2, 1) + relay(7, 3, 2)
+    plan += [("units",), ("gates",), ("tokens", 4)]
+    plan += shared(1, 0, 3, 2) + [("add", 0, True)] + relay(6, 3, 2)
+    plan += shared(5, 4) + [("add", 2, False)] + relay(7, 1) + relay(6, 1) + relay(7, 0)
+    plan += [("add", 4, False)] + shared(7, 6) + [("add", 6, False)]
+    return plan
+
+
 def fused_kernel(n_dp, n_ex, *refs):
     shares, owner, table, dense, tokens, cotangent, mixed, token_grad, grads, *refs = refs
     side, full, picked, weights, pre, mult, own_acts, far_acts, *refs = refs
-    data, recv, swap, upper, order_ref, act_rows, grad_rows, gates, gate_col, both_col, *refs = refs
+    data, recv, swap, relay, upper, order_ref, act_rows, grad_rows, gates, gate_col, both_col, *refs = refs
     load_sem, gate_sem, row_send, row_recv, fwd_send, fwd_recv, tok_send, tok_recv, *refs = refs
-    act_sem, halve_send, halve_recv, swap_sem, out_sem = refs
+    act_sem, halve_send, halve_recv, swap_sem, out_sem, relay_send, relay_recv = refs
 
     row, col = lax.axis_index("dp"), lax.axis_index("expert")
     me = row * n_ex + col
@@ -375,7 +406,7 @@
     def ranks(mask):
         return jnp.dot(mask.astype(BF16), upper[...], preferred_element_type=F32)
 
-    def send_rows(mask):
+    def pick_rows(mask):
         target = flip_mask(col, mask)
         local = shares[owner[target]] - row * block_units
         inside = jnp.logical_and(local >= 0, local < block_units)
@@ -398,73 +429,87 @@
             rows = jnp.dot(hot, side[k], preferred_element_type=F32).astype(BF16)
             for g in range(n_dp):
                 picked[mask * n_dp + g, k] = rows[g * padded : g * padded + pick, :]
-        for turn in range(n_dp):
-            g = flip_mask(row, turn)
-
-            def one(k, carry, g=g, turn=turn):
-                source = picked.at[mask * n_dp + g, k]
-                start = pl.multiple_of((g % 2 * n_dp + row) * padded, padded)
-                target_ref = weights.at[
-                    k,
-                    pl.ds(start, pick),
-                    pl.ds(pl.multiple_of(col * feat, feat), feat),
-                ]
-                if mask == 0 and turn == 0:
-                    pltpu.make_async_copy(source, target_ref, row_recv.at[col]).start()
-                else:
-                    remote(
-                        source,
-                        target_ref,
-                        row_send.at[0],
-                        row_recv.at[col],
-                        {"dp": g, "expert": target},
-                    ).start()
+
+    def spot_of(holder, g, source_col):
+        start = pl.multiple_of((g % 2 * n_dp + holder) * padded, padded)
+        return weights.at[
+            :, pl.ds(start, pick), pl.ds(pl.multiple_of(source_col * feat, feat), feat)
+        ]
+
+    def send_rows(mask, turn):
+        z_mask, slot = mask // 2, mask % 2 * n_dp + turn
+        g = flip_mask(row, turn)
+        source = picked.at[mask * n_dp + g]
+        if mask == 0 and turn == 0:
+            pltpu.make_async_copy(source, spot_of(row, row, col), row_recv.at[col]).start()
+        elif z_mask and slot:
+            remote(
+                source,
+                relay.at[z_mask - 1, slot - 1],
+                row_send.at[0],
+                relay_recv.at[z_mask - 1, slot - 1],
+                {"dp": row, "expert": flip_mask(col, 2 * z_mask)},
+            ).start()
+        else:
+            remote(
+                source,
+                spot_of(row, g, col),
+                row_send.at[0],
+                row_recv.at[col],
+                {"dp": g, "expert": flip_mask(col, mask)},
+            ).start()
+
+    def pass_rows(mask, turn):
+        z_mask, slot = mask // 2, mask % 2 * n_dp + turn
+        source = relay.at[z_mask - 1, slot - 1]
+        source_col = flip_mask(col, 2 * z_mask)
+        g = flip_mask(row, turn)
+        wait(source, relay_recv.at[z_mask - 1, slot - 1])
+        remote(
+            source,
+            spot_of(row, g, source_col),
+            relay_send.at[0],
+            row_recv.at[source_col],
+            {"dp": g, "expert": flip_mask(col, mask % 2)},
+        ).start()
+
+    def step_tokens(step):
+        wait_tokens(step - 1, tok_recv)
+        send_tokens(step)
+
+    def place_units():
+        mine = shares[owner[col], pl.ds(row, 1), :]
+        at_row = jnp.zeros((1, share), F32)
+        for b in range(n_dp):
+            inside = jnp.logical_and(mine >= b * block_units, mine < (b + 1) * block_units)
+            at_row = at_row + jnp.where(inside, ranks(inside) + float(b * padded), 0.0)
+        diagonal = lax.broadcasted_iota(jnp.int32, (share, share), 0) == lax.broadcasted_iota(
+            jnp.int32, (share, share), 1
+        )
+        at_col = jnp.sum(jnp.where(diagonal, at_row, 0.0), axis=1, keepdims=True)
+        order_ref[...] = (
+            at_col.astype(jnp.int32) == lax.broadcasted_iota(jnp.int32, (share, half_units), 1)
+        ).astype(BF16)
+
+    def place_gates():
+        wait(table.at[pl.ds(0, n_ex - 1)], gate_sem.at[0])
+        wait(gates, gate_sem.at[1])
+        copy_id = owner[col] // (n_ex // 2)
+        lanes = lax.broadcasted_iota(jnp.int32, (quarter, tok), 1)
+        below = lax.broadcasted_iota(jnp.int32, (quarter, tok), 0)
+        for xq in range(n_x):
+
+            def column(block, carry, xq=xq):
+                hit = lanes == below + (xq * 2 + core) * quarter
+                value = jnp.sum(jnp.where(hit, gates[block], 0.0), axis=1, keepdims=True)
+                value = jnp.broadcast_to(value, (quarter, 128))
+                blocks = jnp.full((quarter, 128), block * 2 // n_ex, jnp.int32)
+                rows = pl.ds(pl.multiple_of((xq * n_ex + block) * quarter, quarter), quarter)
+                gate_col[rows, :] = value
+                both_col[rows, :] = value + (blocks == copy_id).astype(F32)
                 return carry
 
-            lax.fori_loop(0, 3, one, 0)
-
-    far, near = [m for m in range(n_ex) if m >= n_ex // 2], [m for m in range(1, n_ex // 2)] + [0]
-    masks = [m for pair in zip(far, near) for m in pair]
-    per_step = 2
-    for step in range(bits - 1):
-        for mask in masks[step * per_step : (step + 1) * per_step]:
-            send_rows(mask)
-        wait_tokens(step, tok_recv)
-        send_tokens(step + 1)
-    for mask in masks[(bits - 1) * per_step :]:
-        send_rows(mask)
-
-    mine = shares[owner[col], pl.ds(row, 1), :]
-    at_row = jnp.zeros((1, share), F32)
-    for b in range(n_dp):
-        inside = jnp.logical_and(mine >= b * block_units, mine < (b + 1) * block_units)
-        at_row = at_row + jnp.where(inside, ranks(inside) + float(b * padded), 0.0)
-    diagonal = lax.broadcasted_iota(jnp.int32, (share, share), 0) == lax.broadcasted_iota(
-        jnp.int32, (share, share), 1
-    )
-    at_col = jnp.sum(jnp.where(diagonal, at_row, 0.0), axis=1, keepdims=True)
-    order_ref[...] = (
-        at_col.astype(jnp.int32) == lax.broadcasted_iota(jnp.int32, (share, half_units), 1)
-    ).astype(BF16)
-
-    wait(table.at[pl.ds(0, n_ex - 1)], gate_sem.at[0])
-    wait(gates, gate_sem.at[1])
-    copy_id = owner[col] // (n_ex // 2)
-    lanes = lax.broadcasted_iota(jnp.int32, (quarter, tok), 1)
-    below = lax.broadcasted_iota(jnp.int32, (quarter, tok), 0)
-    for xq in range(n_x):
-
-        def column(block, carry, xq=xq):
-            hit = lanes == below + (xq * 2 + core) * quarter
-            value = jnp.sum(jnp.where(hit, gates[block], 0.0), axis=1, keepdims=True)
-            value = jnp.broadcast_to(value, (quarter, 128))
-            blocks = jnp.full((quarter, 128), block * 2 // n_ex, jnp.int32)
-            rows = pl.ds(pl.multiple_of((xq * n_ex + block) * quarter, quarter), quarter)
-            gate_col[rows, :] = value
-            both_col[rows, :] = value + (blocks == copy_id).astype(F32)
-            return carry
-
-        lax.fori_loop(0, n_ex, column, 0)
+            lax.fori_loop(0, n_ex, column, 0)
 
     my_rows = pl.ds(pl.multiple_of(core * half, half), half)
     my_units = pl.ds(pl.multiple_of(core * half_units, half_units), half_units)
@@ -484,13 +529,15 @@
             remote(view, view, fwd_send.at[0], fwd_recv.at[f], sibling).start()
 
     def accumulate(mask, first):
-        f = flip_mask(col, mask)
-        wait(weights.at[:, far_units, columns(mask)], fwd_recv.at[f])
+        for near in range(2):
+            f = flip_mask(col, mask + near)
+            wait(weights.at[:, far_units, columns(mask + near)], fwd_recv.at[f])
+        both = pl.ds(pl.multiple_of(flip_mask(col, mask) // 2 * (2 * feat), 2 * feat), 2 * feat)
 
         def one(index, carry):
             k, n = index // tiles, index % tiles
             units = pl.ds(pl.multiple_of(n * n_tile, n_tile), n_tile)
-            value = dot(full[k // 2, my_rows, columns(mask)], weights[k, units, columns(mask)], 1, 1)
+            value = dot(full[k // 2, my_rows, both], weights[k, units, both], 1, 1)
             if first:
                 pre[k, :, units] = value
             else:
@@ -499,11 +546,18 @@
 
         lax.fori_loop(0, 3 * tiles, one, 0)
 
-    for at, mask in enumerate(masks):
-        forward(mask)
-        if at:
-            accumulate(masks[at - 1], at == 1)
-    accumulate(masks[-1], False)
+    acts = {
+        "pick": pick_rows,
+        "send": send_rows,
+        "pass": pass_rows,
+        "tokens": step_tokens,
+        "units": place_units,
+        "gates": place_gates,
+        "share": forward,
+        "add": accumulate,
+    }
+    for name, *where in gather_plan():
+        acts[name](*where)
 
     r_tile = 32
 
@@ -713,6 +767,7 @@
     for k in range(3):
         pltpu.make_async_copy(grad_rows.at[k], grads.at[0, k], out_sem.at[k]).wait()
     wait(picked.at[pl.ds(0, n_dp * n_ex - 1)], row_send.at[0])
+    wait(relay, relay_send.at[0])
     wait(weights.at[:, my_units, :], fwd_send.at[0])
     for step in range(bits):
         wait_tokens(step, tok_send)
@@ -762,6 +817,7 @@
             pltpu.VMEM((streams, chips, r_rows, chunk), BF16),
             pltpu.VMEM((streams, chips - 1, r_rows, chunk), BF16),
             pltpu.VMEM((2, streams // 4, r_rows, chunk), BF16),
+            pltpu.VMEM((n_ex // 2 - 1, 2 * n_dp - 1, 3, pick, feat), BF16),
             pltpu.VMEM((share, share), BF16),
             pltpu.VMEM((share, half_units), BF16),
             pltpu.VMEM((share, n_ex * tok), BF16),
@@ -782,6 +838,8 @@
             pltpu.SemaphoreType.DMA((streams, bits - 1)),
             pltpu.SemaphoreType.DMA((2,)),
             pltpu.SemaphoreType.DMA((3,)),
+            pltpu.SemaphoreType.DMA((1,)),
+            pltpu.SemaphoreType.DMA((n_ex // 2 - 1, 2 * n_dp - 1)),
         ],
         compiler_params=pltpu.CompilerParams(
             collective_id=2, has_side_effects=True, vmem_limit_bytes=63 << 20

time: 197 us -> 180 us (0.914)
  Pallas kernels: 185 us -> 168 us
    pallas_call x1, Pallas kernels: 185 us -> 168 us  [fused_step(): pl.pallas_call(functools.partial(fused_kernel, n_dp, n_ex), out_shape=[ja...]
where the time goes in v2:
time: 180 us; the launch traced here: 179 us
  Pallas kernels  168 us (93%)
  local copies, waits for them, and re-layouts  9.57 us (5%)
    pallas_call x1, Pallas kernels, fused_step(): pl.pallas_call(functools.partial(fused_kernel, n_dp, n_ex), out_shape=[ja...  168 us
    unnamed x3, local copies, waits for them, and re-layouts  8.04 us

profile of v2, /device:TPU:0, one launch (start us, length us, event | category | flops | bytes accessed | tf_op | source)
XLA Modules:
  0.0 179.2 jit_solution(6288129475919239643)
XLA Ops:
  0.6 1.3 select_reduce_fusion
  1.9 1.5 reshape.14.refs_0_
  3.5 167.7 %fused_step.1 = (bf16[128,512]{1,0:T(8,128)(2,1)}, bf16[128,512]{1,0:T(8,128)(2,1)}, bf16[1,3,352,2048]{3,2,1,0:T(8,128)(2,1)}) custom-call(s32[8,4,352]{2,1,0:T(4,128)} %reshape.14.refs_0_, s32[8]{0:T(128)} %refs_1_.1, f32[8,1,128]{2,1,0:T(1,128)} %bitcast.1, bf16[3,1408,256]{2,1,0:T(8,128)(2,1)} %refs_3_.1, bf16[128,2048]{1,0:T(8,128)(2,1)} %refs_4_.1, ...), custom_call_target="tpu_custom_call" | custom-call | tf_op jit(solution)/shard_map/fused_step/pallas_call | solution.py:792
  171.2 1.6 copy.15
  172.7 1.6 copy.16
  174.3 4.9 %copy.17 = bf16[1,3,352,2048]{3,2,1,0:T(8,128)(2,1)} copy(bf16[1,3,352,2048]{3,2,1,0:T(8,128)(2,1)} %get-tuple-element.8) | data formatting | bytes 8650752

commit v3 on v2

--- a/solution.py
+++ b/solution.py
@@ -289,8 +289,8 @@
 
 
 def fused_kernel(n_dp, n_ex, *refs):
-    shares, owner, table, dense, tokens, cotangent, mixed, token_grad, grads, *refs = refs
-    side, full, picked, weights, pre, mult, own_acts, far_acts, *refs = refs
+    perm, owner, routes, route_gates, dense, tokens, cotangent, mixed, token_grad, grads, *refs = refs
+    side, full, picked, weights, pre, mult, own_acts, far_acts, table, *refs = refs
     data, recv, swap, relay, upper, order_ref, act_rows, grad_rows, gates, gate_col, both_col, *refs = refs
     load_sem, gate_sem, row_send, row_recv, fwd_send, fwd_recv, tok_send, tok_recv, *refs = refs
     act_sem, halve_send, halve_recv, swap_sem, out_sem, relay_send, relay_recv = refs
@@ -301,7 +301,9 @@
     n_x = n_dp // 2
     chip = spot_x * n_ex + col
     block_units, feat = side.shape[1:]
-    pick, share = picked.shape[2], shares.shape[2]
+    pick, share = picked.shape[2], upper.shape[0]
+    slabs = n_ex // 2
+    slab_units = share * n_dp
     padded = weights.shape[1] // (2 * n_dp)
     half_units = n_dp * padded
     width = full.shape[2]
@@ -338,7 +340,9 @@
             load_sem.at[at],
         ).start()
     pltpu.make_async_copy(dense, side, load_sem.at[2]).start()
-    pltpu.make_async_copy(table.at[col], gates.at[col], gate_sem.at[1]).start()
+    for e in range(n_ex):
+        chosen = jnp.where(routes[...] == e, route_gates[...], 0.0)
+        table[e] = jnp.sum(chosen, axis=0, keepdims=True)
 
     if padded > pick:
         for k in range(3):
@@ -355,10 +359,6 @@
         lax.broadcasted_iota(jnp.int32, (share, share), 0)
         < lax.broadcasted_iota(jnp.int32, (share, share), 1)
     ).astype(BF16)
-    pl.semaphore_wait(barrier, n_dp * n_ex - 1)
-
-    for at in range(2):
-        wait(place(at, me), load_sem.at[at])
 
     ex_order = list(range(ex_bits - 1, -1, -1))
     dp_order = [ex_bits + bit for bit in range(dp_bits - 1, -1, -1)]
@@ -391,24 +391,23 @@
         for at in range(2):
             wait(full.at[at, pl.ds(0, (1 << step) * quarter), :], sem.at[at, step])
 
-    send_tokens(0)
-    for mask in range(1, n_ex):
-        device = flip_mask(me, mask)
-        remote(
-            table.at[device % n_ex],
-            gates.at[col],
-            gate_sem.at[0],
-            gate_sem.at[1],
-            peer(device, n_ex),
-        ).start()
-    wait(side, load_sem.at[2])
-
     def ranks(mask):
         return jnp.dot(mask.astype(BF16), upper[...], preferred_element_type=F32)
 
+    def slab_rows(e):
+        owned = jnp.full((1, slab_units), owner[e], jnp.int32)
+        line = jnp.zeros((1, slab_units), jnp.int32)
+        for slab in range(n_ex):
+            start = slab % slabs * slab_units
+            units = perm[slab // slabs : slab // slabs + 1, start : start + slab_units]
+            line = jnp.where(owned == slab, units, line)
+        return jnp.concatenate(
+            [line[:, g * share : (g + 1) * share] for g in range(n_dp)], axis=0
+        )
+
     def pick_rows(mask):
         target = flip_mask(col, mask)
-        local = shares[owner[target]] - row * block_units
+        local = slab_rows(target) - row * block_units
         inside = jnp.logical_and(local >= 0, local < block_units)
         spots = jnp.where(inside, ranks(inside), -1.0)
         values = (local + 1).astype(F32)
@@ -478,7 +477,10 @@
         send_tokens(step)
 
     def place_units():
-        mine = shares[owner[col], pl.ds(row, 1), :]
+        rows = slab_rows(col)
+        mine = rows[:1]
+        for g in range(1, n_dp):
+            mine = jnp.where(row == g, rows[g : g + 1], mine)
         at_row = jnp.zeros((1, share), F32)
         for b in range(n_dp):
             inside = jnp.logical_and(mine >= b * block_units, mine < (b + 1) * block_units)
@@ -494,7 +496,7 @@
     def place_gates():
         wait(table.at[pl.ds(0, n_ex - 1)], gate_sem.at[0])
         wait(gates, gate_sem.at[1])
-        copy_id = owner[col] // (n_ex // 2)
+        copy_id = owner[col] // slabs
         lanes = lax.broadcasted_iota(jnp.int32, (quarter, tok), 1)
         below = lax.broadcasted_iota(jnp.int32, (quarter, tok), 0)
         for xq in range(n_x):
@@ -556,7 +558,25 @@
         "share": forward,
         "add": accumulate,
     }
-    for name, *where in gather_plan():
+    plan = gather_plan()
+    wait(side, load_sem.at[2])
+    pick_rows(*plan[0][1:])
+    pl.semaphore_wait(barrier, n_dp * n_ex - 1)
+
+    for at in range(2):
+        wait(place(at, me), load_sem.at[at])
+    send_tokens(0)
+    pltpu.make_async_copy(table.at[col], gates.at[col], gate_sem.at[1]).start()
+    for mask in range(1, n_ex):
+        device = flip_mask(me, mask)
+        remote(
+            table.at[device % n_ex],
+            gates.at[col],
+            gate_sem.at[0],
+            gate_sem.at[1],
+            peer(device, n_ex),
+        ).start()
+    for name, *where in plan[1:]:
         acts[name](*where)
 
     r_tile = 32
@@ -777,10 +797,12 @@
     wait(swap, swap_sem.at[0])
 
 
-def fused_step(n_dp, n_ex, shares, slab_owner, table, dense_weights, tokens, cotangent):
+def fused_step(
+    n_dp, n_ex, unit_perm, slab_owner, routes, route_gates, dense_weights, tokens, cotangent
+):
     _, block_units, feat = dense_weights.shape
     tok, width = tokens.shape
-    share = shares.shape[2]
+    share = unit_perm.shape[1] // (n_ex // 2) // n_dp
     pick = share // n_dp
     padded = -(-pick // 16) * 16
     half_units, half = n_dp * padded, n_ex * tok // 2
@@ -789,7 +811,7 @@
     streams = 2 * (width // n_x // chunk)
     any_spec, vmem_spec = pl.BlockSpec(memory_space=pl.ANY), pl.BlockSpec(memory_space=pltpu.VMEM)
     r_rows = tok // 2
-    return pl.pallas_call(
+    results = pl.pallas_call(
         functools.partial(fused_kernel, n_dp, n_ex),
         out_shape=[
             jax.ShapeDtypeStruct((tok, width // n_dp), BF16),
@@ -799,6 +821,7 @@
         in_specs=[
             vmem_spec,
             pl.BlockSpec(memory_space=pltpu.SMEM),
+            vmem_spec,
             vmem_spec,
             any_spec,
             any_spec,
@@ -814,6 +837,7 @@
             pltpu.VMEM((3, half, 2 * half_units), BF16),
             pltpu.VMEM((2, 3, half, half_units), BF16),
             pltpu.VMEM((3, half, half_units), BF16),
+            pltpu.VMEM((n_ex, 1, tok), F32),
             pltpu.VMEM((streams, chips, r_rows, chunk), BF16),
             pltpu.VMEM((streams, chips - 1, r_rows, chunk), BF16),
             pltpu.VMEM((2, streams // 4, r_rows, chunk), BF16),
@@ -845,7 +869,44 @@
             collective_id=2, has_side_effects=True, vmem_limit_bytes=63 << 20
         ),
         name="fused_step",
-    )(shares, slab_owner, table.reshape(n_ex, 1, tok), dense_weights, tokens, cotangent)
+    )(unit_perm, slab_owner, routes.T, route_gates.T, dense_weights, tokens, cotangent)
+    pieces = len(publish_rows(share))
+    return pl.pallas_call(
+        publish_kernel,
+        out_shape=[jax.ShapeDtypeStruct(result.shape, result.dtype) for result in results],
+        in_specs=[any_spec] * 3,
+        out_specs=[any_spec] * 3,
+        scratch_shapes=[
+            pltpu.VMEM((2, tok, width // n_dp), BF16),
+            pltpu.VMEM((3, share, width), BF16),
+            pltpu.SemaphoreType.DMA((2, 3 * pieces + 2)),
+        ],
+        compiler_params=pltpu.CompilerParams(vmem_limit_bytes=63 << 20),
+        name="publish",
+    )(*results)
+
+
+def publish_rows(rows):
+    size = -(-rows // 64) * 16
+    return [(start, min(size, rows - start)) for start in range(0, rows, size)]
+
+
+def publish_kernel(mixed, token_grad, grads, mixed_out, token_grad_out, grads_out, small, large, sem):
+    moves = [
+        (mixed, small.at[0], mixed_out),
+        (token_grad, small.at[1], token_grad_out),
+    ]
+    for k in range(3):
+        for start, size in publish_rows(large.shape[1]):
+            rows = pl.ds(start, size)
+            moves.append((grads.at[0, k, rows], large.at[k, rows], grads_out.at[0, k, rows]))
+    for at, (source, middle, _) in enumerate(moves):
+        pltpu.make_async_copy(source, middle, sem.at[0, at]).start()
+    for at, (source, middle, target) in enumerate(moves):
+        pltpu.make_async_copy(source, middle, sem.at[0, at]).wait()
+        pltpu.make_async_copy(middle, target, sem.at[1, at]).start()
+    for at, (_, middle, target) in enumerate(moves):
+        pltpu.make_async_copy(middle, target, sem.at[1, at]).wait()
 
 
 def gather_plain(n_dp, n_ex, row, picked, tokens, cotangent, table):
@@ -884,17 +945,10 @@
     tok, width = tokens.shape
 
     shares = unit_perm.reshape(n_ex, n_dp, share)
-    gate_table = jnp.sum(
-        jnp.where(
-            routes[None, :, :] == lax.broadcasted_iota(jnp.int32, (n_ex, 1, 1), 0),
-            route_gates[None, :, :],
-            0.0,
-        ),
-        axis=2,
-    )
     padded = -(-pick // 16) * 16
     if (
         copies == 2
+        and slab_units % 128 == 0
         and pick % 8 == 0
         and feat % 256 == 0
         and n_dp * padded % 128 == 0
@@ -906,9 +960,25 @@
     ):
         return tuple(
             fused_step(
-                n_dp, n_ex, shares, slab_owner, gate_table, dense_weights, tokens, cotangent
+                n_dp,
+                n_ex,
+                unit_perm,
+                slab_owner,
+                routes,
+                route_gates,
+                dense_weights,
+                tokens,
+                cotangent,
             )
         )
+    gate_table = jnp.sum(
+        jnp.where(
+            routes[None, :, :] == lax.broadcasted_iota(jnp.int32, (n_ex, 1, 1), 0),
+            route_gates[None, :, :],
+            0.0,
+        ),
+        axis=2,
+    )
     dest = jnp.transpose(shares[slab_owner], (1, 0, 2)).reshape(n_dp * n_ex, share)
     mask, rank = block_ranks(dest // block_units, row)
     place = jnp.where(mask, rank, -1)

time: 180 us -> 173 us (0.961)
  local copies, waits for them, and re-layouts: 9.57 us -> 0 us
  Pallas kernels: 168 us -> 172 us
    unnamed x3 -> x0, local copies, waits for them, and re-layouts: 8.04 us -> none
    pallas_call x0 -> x1, Pallas kernels: none -> 4.27 us  [fused_step(): pl.pallas_call(publish_kernel, out_shape=[jax.ShapeDtypeStruct(result.sha...]
where the time goes in v3:
time: 173 us
  Pallas kernels  172 us (99%)
    pallas_call x1, Pallas kernels, fused_step(): pl.pallas_call(functools.partial(fused_kernel, n_dp, n_ex), out_shape=[ja...  168 us
    pallas_call x1, Pallas kernels, fused_step(): pl.pallas_call(publish_kernel, out_shape=[jax.ShapeDtypeStruct(result.sha...  4.27 us

profile of v3, /device:TPU:0, one launch (start us, length us, event | category | flops | bytes accessed | tf_op | source)
XLA Modules:
  0.0 172.9 jit_solution(12008440774934866860)
XLA Ops:
  0.6 167.8 %fused_step.1 = (bf16[128,512]{1,0:T(8,128)(2,1)}, bf16[128,512]{1,0:T(8,128)(2,1)}, bf16[1,3,352,2048]{3,2,1,0:T(8,128)(2,1)}) custom-call(s32[2,5632]{1,0:T(2,128)} %refs_0_.1, s32[8]{0:T(128)} %refs_1_.1, s32[4,128]{1,0:T(4,128)} %bitcast.2, f32[4,128]{1,0:T(4,128)} %bitcast.3, bf16[3,1408,256]{2,1,0:T(8,128)(2,1)} %refs_4_.1, bf16[128,2048]{1,0:T(8,128)(2,1)} %refs_5_.1, ...), custom_call_target="tpu_custom_call" | custom-call | tf_op jit(solution)/shard_map/fused_step/pallas_call | solution.py:814
  168.4 4.3 %publish.1 = (bf16[128,512]{1,0:T(8,128)(2,1)}, bf16[128,512]{1,0:T(8,128)(2,1)}, bf16[1,3,352,2048]{3,2,1,0:T(8,128)(2,1)}) custom-call(bf16[128,512]{1,0:T(8,128)(2,1)} %get-tuple-element.6.mixed, bf16[128,512]{1,0:T(8,128)(2,1)} %get-tuple-element.7.token_grad, bf16[1,3,352,2048]{3,2,1,0:T(8,128)(2,1)} %get-tuple-element.8.grads), custom_call_target="tpu_custom_call" | custom-call | tf_op jit(solution)/shard_map/publish/pallas_call | solution.py:874

commit v4 on v3

--- a/solution.py
+++ b/solution.py
@@ -273,15 +273,15 @@
         return [("share", mask) for mask in masks]
 
     plan = pick(5) + send(5, 3, 2) + pick(1) + send(1, *every) + pick(0) + send(0, *every)
-    plan += send(5, 1, 0) + [("tokens", 1)]
+    plan += send(5, 1, 0) + [("units",), ("tokens", 1)]
     plan += pick(4) + send(4, 3, 2, 1) + pick(3) + send(3, *every) + relay(5, 3, 2)
-    plan += [("tokens", 2)]
+    plan += [("gates",), ("tokens", 2)]
     plan += pick(7) + send(7, 3, 2) + pick(2) + send(2, *every) + relay(5, 1, 0)
     plan += [("tokens", 3)]
     plan += relay(3, *every) + pick(6) + send(4, 0) + send(6, 3, 2) + send(7, 1)
     plan += send(6, 1) + send(7, 0) + send(6, 0)
     plan += relay(4, 3, 2, 1) + relay(2, 3, 2, 1) + relay(7, 3, 2)
-    plan += [("units",), ("gates",), ("tokens", 4)]
+    plan += [("tokens", 4)]
     plan += shared(1, 0, 3, 2) + [("add", 0, True)] + relay(6, 3, 2)
     plan += shared(5, 4) + [("add", 2, False)] + relay(7, 1) + relay(6, 1) + relay(7, 0)
     plan += [("add", 4, False)] + shared(7, 6) + [("add", 6, False)]

time: 173 us -> 173 us (level)
  no operation moved by 1% of the time
where the time goes in v4:
time: 173 us
  Pallas kernels  172 us (99%)
    pallas_call x1, Pallas kernels, fused_step(): pl.pallas_call(functools.partial(fused_kernel, n_dp, n_ex), out_shape=[ja...  168 us
    pallas_call x1, Pallas kernels, fused_step(): pl.pallas_call(publish_kernel, out_shape=[jax.ShapeDtypeStruct(result.sha...  4.27 us

profile of v4, /device:TPU:0, one launch (start us, length us, event | category | flops | bytes accessed | tf_op | source)
XLA Modules:
  0.0 172.8 jit_solution(12271297151915378804)
XLA Ops:
  0.6 167.8 %fused_step.1 = (bf16[128,512]{1,0:T(8,128)(2,1)}, bf16[128,512]{1,0:T(8,128)(2,1)}, bf16[1,3,352,2048]{3,2,1,0:T(8,128)(2,1)}) custom-call(s32[2,5632]{1,0:T(2,128)} %refs_0_.1, s32[8]{0:T(128)} %refs_1_.1, s32[4,128]{1,0:T(4,128)} %bitcast.2, f32[4,128]{1,0:T(4,128)} %bitcast.3, bf16[3,1408,256]{2,1,0:T(8,128)(2,1)} %refs_4_.1, bf16[128,2048]{1,0:T(8,128)(2,1)} %refs_5_.1, ...), custom_call_target="tpu_custom_call" | custom-call | tf_op jit(solution)/shard_map/fused_step/pallas_call | solution.py:814
  168.4 4.3 %publish.1 = (bf16[128,512]{1,0:T(8,128)(2,1)}, bf16[128,512]{1,0:T(8,128)(2,1)}, bf16[1,3,352,2048]{3,2,1,0:T(8,128)(2,1)}) custom-call(bf16[128,512]{1,0:T(8,128)(2,1)} %get-tuple-element.6.mixed, bf16[128,512]{1,0:T(8,128)(2,1)} %get-tuple-element.7.token_grad, bf16[1,3,352,2048]{3,2,1,0:T(8,128)(2,1)} %get-tuple-element.8.grads), custom_call_target="tpu_custom_call" | custom-call | tf_op jit(solution)/shard_map/publish/pallas_call | solution.py:874
